TPU v7x, 32 devices: a whole 2x2x4 slice. The times are simulated.
32 devices in a mesh: groups: 2 (over x), space: 16 (over z, y, core).
Axes of the slice: x: 2, y: 2, z: 4, core: 2. Of those that a mesh axis runs over, the one named last changes fastest.
Arguments:
- signal: float32 [65536, 128], P(('groups', 'space')), parts along dimension 0, may hold values from -12 to 12
- space_tiles: float32 [512, 64, 384], P('space'), may hold values from -0.3125 to 0.3125
- tree_precision: float32 [256, 128], P('groups'), parts along dimension 0, may hold values from -0.5 to 0.5
- send_tiles: int32 [16, 4, 8], P('space'), may hold values from 0 to 31, as said below
- column_tiles: int32 [512, 6], P('space'), may hold values from 0 to 63, as said below
Outputs:
- product: float32 [65536, 128], P(('groups', 'space')), parts along dimension 0
- quad_form: float32 [2], P('groups'), parts along dimension 0
There are 2 independent parts, one for each index of `groups`. A program takes and returns all parts, laid end to end along the dimension named above; an argument that names none is the same for every part. Nothing has to cross between parts.
Inputs may be any that keep to these rules, and one draw needn't show every extreme that they name: `send_tiles`: within one list the tile numbers are distinct; a partition lists tiles only towards neighbours that exist on the grid, from 1 to 8 of them, and some partition lists 8 tiles east and another south; slots past a list's length hold other tiles. `column_tiles`: entry 0 of every tile row is the row's own tile; entries below 32 are the partition's own tiles; an entry 32 + d * 8 + j names slot j of the list received from direction d, and only slots within that list's length.
All inputs are finite; a program needn't handle non-finite values.
Results may differ from a plain program's by a relative error of at most 0.00022.
Values sent between devices are 32-bit elements; how exact they have to be, the bound alone decides.
No kernel may reach another device: no remote copies, remote signals or barrier semaphores. Data moves between devices by JAX's collectives and lax.ppermute only.
A program may use at most 64 MiB of HBM per device.

v0:
```python
import jax
import jax.numpy as jnp
from jax import lax
from jax.sharding import PartitionSpec as P


def from_behind(block, axis, distance):
    devices = range(lax.axis_size(axis))
    route = [(i - distance, i) for i in devices if i - distance in devices]
    return lax.ppermute(block, axis, route)


def receive_lists(tiled, lists, wide):
    offsets = [1, -1, wide, -wide]
    pieces = []
    for direction in range(4):
        outgoing = tiled[lists[direction]]
        pieces.append(from_behind(outgoing, "space", offsets[direction]))
    return jnp.concatenate(pieces, axis=0)


def on_device(signal, space_tiles, tree_precision, send_tiles, column_tiles):
    count = lax.axis_size("space")
    wide = count // 8
    tile_rows = space_tiles.shape[0]
    tile_nodes = space_tiles.shape[1]
    stored = space_tiles.shape[2] // tile_nodes
    species = signal.shape[1]
    tiled = signal.reshape(tile_rows, tile_nodes, species)
    lists = send_tiles[0]
    received = receive_lists(tiled, lists, wide)
    extended = jnp.concatenate([tiled, received], axis=0)
    gathered = extended[column_tiles].reshape(tile_rows, stored * tile_nodes, species)
    spatial = jnp.einsum("rac,rcs->ras", space_tiles, gathered, precision=lax.Precision.HIGHEST)
    spatial = spatial.reshape(tile_rows * tile_nodes, species)
    product = jnp.dot(
        spatial,
        tree_precision.T,
        precision=lax.Precision.HIGHEST,
        preferred_element_type=jnp.float32,
    )
    total = lax.psum(jnp.sum(signal * product), "space")
    scaling = jnp.sqrt(jnp.float32(count * tile_rows * tile_nodes * species))
    return (product, (total / scaling).reshape(1))


def solution(mesh):
    placed = (
        P(("groups", "space"), None),
        P("space", None, None),
        P("groups", None),
        P("space", None, None),
        P("space", None),
    )
    return jax.shard_map(
        on_device,
        mesh=mesh,
        in_specs=placed,
        out_specs=(P(("groups", "space"), None), P("groups")),
        check_vma=False,
    )
```

profile of v0, /device:TPU:0, one launch (start us, length us, event | category | flops | bytes accessed | tf_op | source)
XLA Modules:
  0.0 82.9 jit_solution(9771057362921722270)
XLA Ops:
  0.6 0.0 copy-start
  0.6 0.0 copy-start.3
  0.7 0.9 %fusion.3 = (s32[8]{0:T(128)S(1)}, s32[8]{0:T(128)S(1)}, s32[8]{0:T(128)S(1)}, s32[8]{0:T(128)S(1)}) fusion(s32[1,4,8]{2,1,0:T(4,128)} %param.8), kind=kLoop, calls=%fused_computation.24 | loop fusion | flops 96 | bytes 256 | tf_op jit(solution)/shard_map/select_n | solution.py:17
  1.6 1.9 %gather_fusion.3 = f32[8,64,128]{2,1,0:T(8,128)S(1)} fusion(f32[32,64,128]{2,1,0:T(8,128)} %bitcast.27, s32[1024]{0:T(1024)S(1)} %pad_clamp_fusion.1), kind=kCustom, calls=%fused_computation.3 | custom fusion | bytes 524320 | tf_op jit(solution)/shard_map/gather | solution.py:17
  3.5 1.3 %collective-permute-start.3 = (f32[8,64,128]{2,1,0:T(8,128)S(1)}, f32[8,64,128]{2,1,0:T(8,128)}, u32[]{:S(2)}, u32[]{:S(2)}) collective-permute-start(f32[8,64,128]{2,1,0:T(8,128)S(1)} %gather_fusion.3), channel_id=1, source_target_pairs={{2,0},{3,1},{4,2},{5,3},{6,4},{7,5},{8,6},{9,7},{10,8},{11,9},{12,... | collective-permute-start | bytes 786440 | tf_op jit(solution)/shard_map/ppermute | solution.py:10
  4.8 2.5 %gather_fusion.1 = f32[8,64,128]{2,1,0:T(8,128)} fusion(f32[32,64,128]{2,1,0:T(8,128)} %bitcast.28, s32[1024]{0:T(1024)S(1)} %pad_clamp_fusion.3), kind=kCustom, calls=%fused_computation.1 | custom fusion | bytes 524320 | tf_op jit(solution)/shard_map/gather | solution.py:17
  7.3 1.3 %collective-permute-start.1 = (f32[8,64,128]{2,1,0:T(8,128)}, f32[8,64,128]{2,1,0:T(8,128)}, u32[]{:S(2)}, u32[]{:S(2)}) collective-permute-start(f32[8,64,128]{2,1,0:T(8,128)} %gather_fusion.1), channel_id=1, source_target_pairs={{1,0},{2,1},{3,2},{4,3},{5,4},{6,5},{7,6},{8,7},{9,8},{10,9},{11,1... | collective-permute-start | bytes 786440 | tf_op jit(solution)/shard_map/ppermute | solution.py:10
  8.6 2.5 %gather_fusion = f32[8,64,128]{2,1,0:T(8,128)} fusion(f32[32,64,128]{2,1,0:T(8,128)} %bitcast.29, s32[1024]{0:T(1024)S(1)} %pad_clamp_fusion.4), kind=kCustom, calls=%fused_computation | custom fusion | bytes 524320 | tf_op jit(solution)/shard_map/gather | solution.py:17
  11.0 3.7 %collective-permute-start = (f32[8,64,128]{2,1,0:T(8,128)}, f32[8,64,128]{2,1,0:T(8,128)}, u32[]{:S(2)}, u32[]{:S(2)}) collective-permute-start(f32[8,64,128]{2,1,0:T(8,128)} %gather_fusion), channel_id=1, source_target_pairs={{0,1},{1,2},{2,3},{3,4},{4,5},{5,6},{6,7},{7,8},{8,9},{9,10},{10,1... | collective-permute-start | bytes 786440 | tf_op jit(solution)/shard_map/ppermute | solution.py:10
  14.8 2.5 %gather_fusion.2 = f32[8,64,128]{2,1,0:T(8,128)} fusion(f32[32,64,128]{2,1,0:T(8,128)} %bitcast.30, s32[1024]{0:T(1024)S(1)} %pad_clamp_fusion.2), kind=kCustom, calls=%fused_computation.2 | custom fusion | bytes 524320 | tf_op jit(solution)/shard_map/gather | solution.py:17
  17.3 5.5 %collective-permute-start.2 = (f32[8,64,128]{2,1,0:T(8,128)}, f32[8,64,128]{2,1,0:T(8,128)}, u32[]{:S(2)}, u32[]{:S(2)}) collective-permute-start(f32[8,64,128]{2,1,0:T(8,128)} %gather_fusion.2), channel_id=1, source_target_pairs={{0,2},{1,3},{2,4},{3,5},{4,6},{5,7},{6,8},{7,9},{8,10},{9,11},{10,... | collective-permute-start | bytes 786440 | tf_op jit(solution)/shard_map/ppermute | solution.py:10
  22.8 0.0 copy-done.3
  22.8 2.3 %constant_dynamic-update-slice_fusion.4 = f32[64,64,128]{2,1,0:T(8,128)} fusion(f32[32,64,128]{2,1,0:T(8,128)} %bitcast.31), kind=kLoop, calls=%fused_computation.11 | loop fusion | bytes 2097152
  25.1 0.1 copy.7
  25.2 0.1 reshape.174
  25.3 0.0 collective-permute-done
  25.3 1.7 %constant_dynamic-update-slice_fusion.3 = f32[64,64,128]{2,1,0:T(8,128)} fusion(f32[64,64,128]{2,1,0:T(8,128)} %constant_dynamic-update-slice_fusion.4, f32[8,64,128]{2,1,0:T(8,128)} %collective-permute-done), kind=kLoop, calls=%fused_computation.10 | loop fusion | bytes 524288
  27.0 0.0 collective-permute-done.1
  27.0 1.7 %constant_dynamic-update-slice_fusion.2 = f32[64,64,128]{2,1,0:T(8,128)} fusion(f32[64,64,128]{2,1,0:T(8,128)} %constant_dynamic-update-slice_fusion.3, f32[8,64,128]{2,1,0:T(8,128)} %collective-permute-done.1), kind=kLoop, calls=%fused_computation.9 | loop fusion | bytes 524288
  28.7 0.0 collective-permute-done.2
  28.7 1.7 %constant_dynamic-update-slice_fusion.1 = f32[64,64,128]{2,1,0:T(8,128)} fusion(f32[64,64,128]{2,1,0:T(8,128)} %constant_dynamic-update-slice_fusion.2, f32[8,64,128]{2,1,0:T(8,128)} %collective-permute-done.2), kind=kLoop, calls=%fused_computation.8 | loop fusion | bytes 524288
  30.4 0.0 collective-permute-done.3
  30.4 1.7 %constant_dynamic-update-slice_fusion = f32[64,64,128]{2,1,0:T(8,128)} fusion(f32[64,64,128]{2,1,0:T(8,128)} %constant_dynamic-update-slice_fusion.1, f32[8,64,128]{2,1,0:T(8,128)} %collective-permute-done.3), kind=kLoop, calls=%fused_computation.7 | loop fusion | bytes 524288 | tf_op jit(solution)/shard_map/concatenate | solution.py:32
  32.1 5.2 %gather_fusion.4 = f32[192,64,128]{2,1,0:T(8,128)} fusion(f32[64,64,128]{2,1,0:T(8,128)} %constant_dynamic-update-slice_fusion, s32[1024]{0:T(1024)S(1)} %pad_clamp_fusion), kind=kCustom, calls=%fused_computation.4 | custom fusion | bytes 12583680 | tf_op jit(solution)/shard_map/gather | solution.py:33
  37.3 0.0 copy-done
  37.3 0.0 copy-start.1
  37.3 0.0 copy-start.2
  37.3 6.8 %fusion.4 = f32[32,128,64]{1,2,0:T(8,128)S(1)} fusion(f32[32,384,128]{2,1,0:T(8,128)} %bitcast.26, f32[32,64,384]{2,1,0:T(8,128)S(1)} %copy-done), kind=kOutput, calls=%fused_computation.25 | convolution fusion | flops 1207959552 | bytes 10485760 | tf_op jit(solution)/shard_map/rac,rcs->ras/dot_general | solution.py:34
  44.1 0.0 copy-done.1
  44.1 0.0 copy-done.2
  44.2 2.6 %multiply_reduce_fusion = (f32[]{:T(128)}, f32[2048,128]{1,0:T(8,128)}) fusion(f32[2048,128]{1,0:T(8,128)S(1)} %copy-done.1, f32[2048,128]{1,0:T(8,128)S(1)} %bitcast.32, f32[128,128]{1,0:T(8,128)S(1)} %copy-done.2), kind=kOutput, calls=%fused_computation.5 | convolution fusion | flops 403177472 | bytes 3211268 | tf_op jit(solution)/shard_map/dot_general | solution.py:36
  46.8 34.3 %psum.7 = f32[]{:T(128)} all-reduce(f32[]{:T(128)} %get-tuple-element.6), channel_id=1, replica_groups=mesh['groups'=2,'space'=16] {'space'}, use_global_device_ids=true, to_apply=%region_1.0 | all-reduce | flops 1 | bytes 8 | tf_op jit(solution)/shard_map/psum | solution.py:42
  (6 shorter events, 0.0 us)
Async XLA Ops:
  0.6 36.7 %copy-start = (f32[32,64,384]{2,1,0:T(8,128)S(1)}, f32[32,64,384]{2,1,0:T(8,128)}, u32[]{:S(2)}) copy-start(f32[32,64,384]{2,1,0:T(8,128)} %param.6) | copy-start | bytes 9437188
  0.6 22.1 %copy-start.3 = (s32[32,6]{0,1:T(8,128)S(1)}, s32[32,6]{0,1:T(8,128)}, u32[]{:S(2)}) copy-start(s32[32,6]{0,1:T(8,128)} %param.9) | copy-start | bytes 2308
  3.5 26.9 %collective-permute-start.3 = (f32[8,64,128]{2,1,0:T(8,128)S(1)}, f32[8,64,128]{2,1,0:T(8,128)}, u32[]{:S(2)}, u32[]{:S(2)}) collective-permute-start(f32[8,64,128]{2,1,0:T(8,128)S(1)} %gather_fusion.3), channel_id=1, source_target_pairs={{2,0},{3,1},{4,2},{5,3},{6,4},{7,5},{8,6},{9,7},{10,8},{11,9},{12,... | collective-permute-start | bytes 786440 | tf_op jit(solution)/shard_map/ppermute | solution.py:10
  7.3 19.8 %collective-permute-start.1 = (f32[8,64,128]{2,1,0:T(8,128)}, f32[8,64,128]{2,1,0:T(8,128)}, u32[]{:S(2)}, u32[]{:S(2)}) collective-permute-start(f32[8,64,128]{2,1,0:T(8,128)} %gather_fusion.1), channel_id=1, source_target_pairs={{1,0},{2,1},{3,2},{4,3},{5,4},{6,5},{7,6},{8,7},{9,8},{10,9},{11,1... | collective-permute-start | bytes 786440 | tf_op jit(solution)/shard_map/ppermute | solution.py:10
  11.0 14.3 %collective-permute-start = (f32[8,64,128]{2,1,0:T(8,128)}, f32[8,64,128]{2,1,0:T(8,128)}, u32[]{:S(2)}, u32[]{:S(2)}) collective-permute-start(f32[8,64,128]{2,1,0:T(8,128)} %gather_fusion), channel_id=1, source_target_pairs={{0,1},{1,2},{2,3},{3,4},{4,5},{5,6},{6,7},{7,8},{8,9},{9,10},{10,1... | collective-permute-start | bytes 786440 | tf_op jit(solution)/shard_map/ppermute | solution.py:10
  17.3 11.4 %collective-permute-start.2 = (f32[8,64,128]{2,1,0:T(8,128)}, f32[8,64,128]{2,1,0:T(8,128)}, u32[]{:S(2)}, u32[]{:S(2)}) collective-permute-start(f32[8,64,128]{2,1,0:T(8,128)} %gather_fusion.2), channel_id=1, source_target_pairs={{0,2},{1,3},{2,4},{3,5},{4,6},{5,7},{6,8},{7,9},{8,10},{9,11},{10,... | collective-permute-start | bytes 786440 | tf_op jit(solution)/shard_map/ppermute | solution.py:10
  37.3 6.9 %copy-start.1 = (f32[2048,128]{1,0:T(8,128)S(1)}, f32[2048,128]{1,0:T(8,128)}, u32[]{:S(2)}) copy-start(f32[2048,128]{1,0:T(8,128)} %param.5) | copy-start | bytes 3145732
  37.3 6.9 %copy-start.2 = (f32[128,128]{1,0:T(8,128)S(1)}, f32[128,128]{1,0:T(8,128)}, u32[]{:S(2)}) copy-start(f32[128,128]{1,0:T(8,128)} %param.7) | copy-start | bytes 196612
where the time goes:
time: 83.4 us; the launch traced here: 82.9 us
  blocking collectives  34.3 us (41%)
  local copies, waits for them, and re-layouts  23.8 us (29%)
  starting transfers between devices  11.8 us (14%)
  matrix products  9.46 us (11%)
  between operations  2.52 us (3%)
  other arithmetic  0.92 us (1%)
    psum x1, blocking collectives, on_device(): total = lax.psum(jnp.sum(signal * product), 'space')  34.3 us
    ppermute x4, starting transfers between devices, from_behind(): return lax.ppermute(block, axis, route)  11.8 us
    gather x4, local copies, waits for them, and re-layouts, receive_lists(): outgoing = tiled[lists[direction]]  9.36 us
    unnamed x12, local copies, waits for them, and re-layouts  7.37 us
    dot_general x1, matrix products, on_device(): jnp.einsum('rac,rcs->ras', space_tiles, gathered, precision=lax.Precision...  6.84 us
    gather x1, local copies, waits for them, and re-layouts, on_device(): extended[column_tiles].reshape(tile_rows, stored * tile_nodes, species)  5.2 us
    dot_general x1, matrix products, on_device(): jnp.dot(spatial, tree_precision.T, precision=lax.Precision.HIGHEST, prefe...  2.62 us
    concatenate x1, local copies, waits for them, and re-layouts, on_device(): extended = jnp.concatenate([tiled, received], axis=0)  1.71 us
  transfers between devices with their start and end apart: 4, of which 0 were waited for; matrix products, arithmetic and copies ran while one was open for 18% of the time, Pallas kernels for 0%

commit v1 on v0

v1 whole, which is shorter than its diff:
```python
import math

import jax
import jax.numpy as jnp
from jax import lax
from jax.experimental import pallas as pl
from jax.experimental.pallas import tpu as pltpu
from jax.sharding import PartitionSpec as P

ROWS = 8
ANY = pl.BlockSpec(memory_space=pl.ANY)
SMEM = pl.BlockSpec(memory_space=pltpu.SMEM)
VMEM = pl.BlockSpec(memory_space=pltpu.VMEM)
PARAMS = pltpu.CompilerParams(vmem_limit_bytes=40 * 1024 * 1024)


def split(x):
    high = x.astype(jnp.bfloat16)
    return high, (x - high.astype(jnp.float32)).astype(jnp.bfloat16)


def stacked(x):
    return jnp.concatenate(split(x), axis=0)


def side_by_side(x):
    return jnp.concatenate(split(x), axis=1)


def dot(a, b, dims):
    return lax.dot_general(a, b, (dims, ((), ())), preferred_element_type=jnp.float32)


def quarters(s):
    rows, lanes = s.shape[0] // 2, s.shape[1] // 2
    return (s[rows:, lanes:] + s[rows:, :lanes]) + s[:rows, lanes:] + s[:rows, :lanes]


def slot_of(column, own, cap, merged):
    entry = column - own
    if merged:
        return jnp.where(entry < 2 * cap, entry % cap, entry - cap)
    return entry


def pick(lists, tiled, wide, merged):
    cap = lists.shape[2]
    count = 3 if merged else 4
    shape = jax.ShapeDtypeStruct((cap,) + tiled.shape[1:], tiled.dtype)

    def kernel(lists_ref, tiled_ref, *rest):
        outs, sems = rest[:count], rest[count]
        if merged:
            column = lax.axis_index("space") % wide
            directions = [jnp.where(column == 0, 0, 1), 2, 3]
        else:
            directions = [0, 1, 2, 3]
        copies = []
        for i in (2, 1, 0) if merged else range(count):
            for j in range(cap):
                tile = lists_ref[0, directions[i], j]
                copies.append(pltpu.make_async_copy(tiled_ref.at[tile], outs[i].at[j], sems.at[i, j]))
                copies[-1].start()
        for copy in copies:
            copy.wait()

    return pl.pallas_call(
        kernel,
        out_shape=[shape] * count,
        in_specs=[SMEM, ANY],
        out_specs=[ANY] * count,
        scratch_shapes=[pltpu.SemaphoreType.DMA((count, cap))],
        name="pick",
    )(lists, tiled)


def exchange(outgoing, wide, merged):
    count = lax.axis_size("space")
    if merged:
        routes = [[(i, i ^ 1) for i in range(count)]]
    else:
        routes = [
            [(i - 1, i) for i in range(count) if i % wide > 0],
            [(i + 1, i) for i in range(count) if i % wide < wide - 1],
        ]
    routes.append([(i - wide, i) for i in range(wide, count)])
    routes.append([(i + wide, i) for i in range(count - wide)])
    return [lax.ppermute(o, "space", r) for o, r in zip(outgoing, routes)]


def local_part(columns, tiled, space_tiles, tree, slots, cap, merged):
    own, nodes, species = tiled.shape
    stored = columns.shape[0]
    wide_k = stored * nodes
    chunk = 4

    def kernel(columns_ref, x_ref, a_ref, tree_ref, product_ref, v_ref, quad_ref, xs_ref, z_ref, sp_ref):
        for c in range(0, own, chunk):
            x = x_ref[c : c + chunk].reshape(chunk * nodes, species)
            xs_ref[c : c + chunk] = side_by_side(x).reshape(chunk, nodes, 2 * species)
        xs_ref[own] = jnp.zeros((nodes, 2 * species), jnp.bfloat16)
        v_ref[...] = jnp.zeros(v_ref.shape, jnp.float32)
        tree_rows = stacked(tree_ref[...])
        tree_lanes = side_by_side(tree_ref[...])

        def row(t, _):
            tiles = []
            for k in range(stored):
                column = columns_ref[k, t]
                tiles.append(xs_ref[jnp.where(column < own, column, own)])
            gathered = jnp.concatenate(tiles, axis=0)
            sp_ref[t] = quarters(dot(stacked(a_ref[t]), gathered, ((1,), (0,))))
            return 0

        lax.fori_loop(0, own, row, 0, unroll=2)

        quad = jnp.zeros((8, species), jnp.float32)
        for c in range(0, own, chunk):
            xs = xs_ref[c : c + chunk].reshape(chunk * nodes, 2 * species)
            x = jnp.concatenate([xs[:, :species], xs[:, species:]], axis=0)
            z = quarters(dot(x, tree_lanes, ((1,), (0,))))
            z_ref[c : c + chunk] = z.reshape(chunk, nodes, species)
            spatial = sp_ref[c : c + chunk].reshape(chunk * nodes, species)
            product = quarters(dot(stacked(spatial), tree_rows, ((1,), (1,))))
            product_ref[c : c + chunk] = product.reshape(chunk, nodes, species)
            quad = quad + (z * spatial).reshape(-1, 8, species).sum(axis=0)
        quad_ref[...] = quad

        def remote_row(t, _):
            columns = [columns_ref[k, t] for k in range(stored)]
            last = columns[0]
            for column in columns[1:]:
                last = jnp.maximum(last, column)

            @pl.when(last >= own)
            def _():
                z = side_by_side(z_ref[t])
                w = dot(stacked(a_ref[t]), jnp.concatenate([z, z], axis=0), ((0,), (0,)))
                w = w[:, species:] + w[:, :species]
                for k in range(stored):

                    @pl.when(columns[k] >= own)
                    def _():
                        slot = slot_of(columns[k], own, cap, merged)
                        v_ref[slot] += w[k * nodes : (k + 1) * nodes]

            return 0

        lax.fori_loop(0, own, remote_row, 0)

    return pl.pallas_call(
        kernel,
        out_shape=[
            jax.ShapeDtypeStruct(tiled.shape, jnp.float32),
            jax.ShapeDtypeStruct((slots, nodes, species), jnp.float32),
            jax.ShapeDtypeStruct((8, species), jnp.float32),
        ],
        in_specs=[SMEM, VMEM, VMEM, VMEM],
        out_specs=[VMEM, VMEM, VMEM],
        scratch_shapes=[
            pltpu.VMEM((own + 1, nodes, 2 * species), jnp.bfloat16),
            pltpu.VMEM(tiled.shape, jnp.float32),
            pltpu.VMEM(tiled.shape, jnp.float32),
        ],
        compiler_params=PARAMS,
        name="local_part",
    )(columns, tiled, space_tiles, tree)


def remote_quad(v, received, quad, count):
    species = v.shape[2]
    cap = received[0].shape[0]

    def kernel(v_ref, quad_ref, *rest):
        parts, out_ref = rest[:-1], rest[-1]
        total = quad_ref[...]
        for i, part in enumerate(parts):
            for j in range(cap):
                total = total + (v_ref[i * cap + j] * part[j]).reshape(-1, 8, species).sum(axis=0)
        total = total.sum(axis=0, keepdims=True)
        for i in range(count):
            out_ref[i] = total

    return pl.pallas_call(
        kernel,
        out_shape=jax.ShapeDtypeStruct((count, 1, species), jnp.float32),
        in_specs=[VMEM] * (2 + len(received)),
        out_specs=VMEM,
        compiler_params=PARAMS,
        name="remote_quad",
    )(v, quad, *received)


def remote_part(columns, space_tiles, tree, product, received, sums, scale, merged):
    own, nodes, species = product.shape
    stored = columns.shape[0]
    cap = received[0].shape[0]
    slots = len(received) * cap
    groups = len(received)

    def kernel(columns_ref, tree_ref, sums_ref, a_hbm, product_hbm, *rest):
        parts = rest[:groups]
        out_hbm, quad_ref, x_ref, xs_ref, a_ref, p_ref, x_sem, a_sem, p_sem, o_sem = rest[groups:]
        copies = [pltpu.make_async_copy(parts[i], x_ref.at[pl.ds(i * cap, cap)], x_sem.at[i]) for i in range(groups)]
        for copy in copies:
            copy.start()

        def load_a(t):
            return pltpu.make_async_copy(a_hbm.at[t], a_ref.at[t], a_sem.at[t])

        def load_p(t):
            return pltpu.make_async_copy(product_hbm.at[t], p_ref.at[t], p_sem.at[t])

        def store_p(t):
            return pltpu.make_async_copy(p_ref.at[t], out_hbm.at[t], o_sem.at[t])

        def last_column(t):
            last = columns_ref[0, t]
            for k in range(1, stored):
                last = jnp.maximum(last, columns_ref[k, t])
            return last

        def each_remote(step):
            def body(t, _):
                @pl.when(last_column(t) >= own)
                def _():
                    step(t)

                return 0

            lax.fori_loop(0, own, body, 0)

        def fetch(t):
            load_a(t).start()
            load_p(t).start()

        each_remote(fetch)
        quad_ref[0] = jnp.sum(sums_ref[...]) * scale
        tree_rows = stacked(tree_ref[...])
        xs_ref[slots] = jnp.zeros((nodes, 2 * species), jnp.bfloat16)
        for i, copy in enumerate(copies):
            copy.wait()
            x = x_ref[i * cap : (i + 1) * cap].reshape(cap * nodes, species)
            xs_ref[i * cap : (i + 1) * cap] = side_by_side(x).reshape(cap, nodes, 2 * species)

        def work(t):
            tiles = []
            for k in range(stored):
                column = columns_ref[k, t]
                slot = slot_of(column, own, cap, merged)
                tiles.append(xs_ref[jnp.where(column < own, slots, slot)])
            load_a(t).wait()
            load_p(t).wait()
            spatial = quarters(dot(stacked(a_ref[t]), jnp.concatenate(tiles, axis=0), ((1,), (0,))))
            p_ref[t] += quarters(dot(stacked(spatial), tree_rows, ((1,), (1,))))
            store_p(t).start()

        each_remote(work)
        each_remote(lambda t: store_p(t).wait())

    return pl.pallas_call(
        kernel,
        out_shape=[jax.ShapeDtypeStruct(product.shape, jnp.float32), jax.ShapeDtypeStruct((1,), jnp.float32)],
        in_specs=[SMEM, VMEM, VMEM, ANY, ANY] + [ANY] * groups,
        out_specs=[ANY, SMEM],
        scratch_shapes=[
            pltpu.VMEM((slots, nodes, species), jnp.float32),
            pltpu.VMEM((slots + 1, nodes, 2 * species), jnp.bfloat16),
            pltpu.VMEM(space_tiles.shape, jnp.float32),
            pltpu.VMEM(product.shape, jnp.float32),
            pltpu.SemaphoreType.DMA((groups,)),
            pltpu.SemaphoreType.DMA((own,)),
            pltpu.SemaphoreType.DMA((own,)),
            pltpu.SemaphoreType.DMA((own,)),
        ],
        input_output_aliases={4: 0},
        compiler_params=PARAMS,
        name="remote_part",
    )(columns, tree, sums, space_tiles, product, *received)


def on_device(signal, space_tiles, tree_precision, send_tiles, column_tiles):
    count = lax.axis_size("space")
    wide = count // ROWS
    merged = wide == 2
    tile_rows, tile_nodes = space_tiles.shape[:2]
    species = signal.shape[1]
    cap = send_tiles.shape[2]
    tiled = signal.reshape(tile_rows, tile_nodes, species)
    columns = column_tiles.T
    outgoing = pick(send_tiles, tiled, wide, merged)
    received = exchange(outgoing, wide, merged)
    slots = len(received) * cap
    product, v, quad = local_part(columns, tiled, space_tiles, tree_precision, slots, cap, merged)
    shares = remote_quad(v, received, quad, count)
    sums = lax.all_to_all(shares, "space", 0, 0)
    scale = 1.0 / math.sqrt(count * tile_rows * tile_nodes * species)
    product, total = remote_part(columns, space_tiles, tree_precision, product, received, sums, scale, merged)
    return product.reshape(signal.shape), total


def solution(mesh):
    placed = (
        P(("groups", "space"), None),
        P("space", None, None),
        P("groups", None),
        P("space", None, None),
        P("space", None),
    )
    return jax.shard_map(
        on_device,
        mesh=mesh,
        in_specs=placed,
        out_specs=(P(("groups", "space"), None), P("groups")),
        check_vma=False,
    )
```

time: 83.4 us -> 68.9 us (0.83)
  Pallas kernels: 0 us -> 44 us
  blocking collectives: 34.3 us -> 13.3 us
  local copies, waits for them, and re-layouts: 23.8 us -> 4.64 us
  matrix products: 9.46 us -> 0 us
  starting transfers between devices: 11.8 us -> 6.26 us
  between operations: 2.52 us -> 0.68 us
  other arithmetic: 0.92 us -> 0 us
    pallas_call x0 -> x4, Pallas kernels: none -> 44 us  [the longest x1 25.8 us: pick(): pl.pallas_call(kernel, out_shape=[shape] * count, in_specs=[SMEM, ANY], o...]
    psum x1 -> x0, blocking collectives: 34.3 us -> none  [on_device(): total = lax.psum(jnp.sum(signal * product), 'space')]
    gather x5 -> x0, local copies, waits for them, and re-layouts: 14.6 us -> none  [the longest x4 9.36 us: receive_lists(): outgoing = tiled[lists[direction]]]
    all_to_all x0 -> x1, blocking collectives: none -> 13.3 us  [on_device(): sums = lax.all_to_all(shares, 'space', 0, 0)]
    dot_general x2 -> x0, matrix products: 9.46 us -> none  [the longest x1 6.84 us: on_device(): jnp.einsum('rac,rcs->ras', space_tiles, gathered, precision=lax.Precision...]
    ppermute x4 -> x3, starting transfers between devices: 11.8 us -> 6.26 us  [exchange(): return [lax.ppermute(o, 'space', r) for o, r in zip(outgoing, routes)]]
    unnamed x12, local copies, waits for them, and re-layouts: 7.37 us -> 4.64 us
    concatenate x1 -> x0, local copies, waits for them, and re-layouts: 1.71 us -> none  [on_device(): extended = jnp.concatenate([tiled, received], axis=0)]
  transfers between devices with their start and end apart: 4 -> 3, of which waited for: 0 -> 0; matrix products, arithmetic and copies ran while one was open for 18% -> 0% of each run, Pallas kernels for 0% -> 14%
where the time goes in v1:
time: 68.9 us
  Pallas kernels  44 us (64%)
  blocking collectives  13.3 us (19%)
  starting transfers between devices  6.26 us (9%)
  local copies, waits for them, and re-layouts  4.64 us (7%)
    pallas_call x1, Pallas kernels, pick(): pl.pallas_call(kernel, out_shape=[shape] * count, in_specs=[SMEM, ANY], o...  25.8 us
    all_to_all x1, blocking collectives, on_device(): sums = lax.all_to_all(shares, 'space', 0, 0)  13.3 us
    pallas_call x1, Pallas kernels, local_part(): pl.pallas_call(kernel, out_shape=[jax.ShapeDtypeStruct(tiled.shape, jnp.f...  9.81 us
    pallas_call x1, Pallas kernels, remote_part(): pl.pallas_call(kernel, out_shape=[jax.ShapeDtypeStruct(product.shape, jnp...  8.29 us
    ppermute x3, starting transfers between devices, exchange(): return [lax.ppermute(o, 'space', r) for o, r in zip(outgoing, routes)]  6.26 us
    unnamed x12, local copies, waits for them, and re-layouts  4.64 us
  transfers between devices with their start and end apart: 3, of which 0 were waited for; matrix products, arithmetic and copies ran while one was open for 0% of the time, Pallas kernels for 14%

profile of v1, /device:TPU:0, one launch (start us, length us, event | category | flops | bytes accessed | tf_op | source)
XLA Modules:
  0.0 68.9 jit_solution(7600171034291434039)
XLA Ops:
  0.6 25.8 %pick.1 = (f32[8,64,128]{2,1,0:T(8,128)}, f32[8,64,128]{2,1,0:T(8,128)}, f32[8,64,128]{2,1,0:T(8,128)}) custom-call(s32[1,4,8]{2,1,0:T(4,128)} %lists_ref.1, f32[32,64,128]{2,1,0:T(8,128)} %bitcast.3), custom_call_target="tpu_custom_call" | custom-call | tf_op jit(solution)/shard_map/pick/pallas_call | solution.py:67
  26.5 0.0 copy-start.5
  26.5 0.5 collective-permute-start
  27.0 4.4 %collective-permute-start.1 = (f32[8,64,128]{2,1,0:T(8,128)}, f32[8,64,128]{2,1,0:T(8,128)S(1)}, u32[]{:S(2)}, u32[]{:S(2)}) collective-permute-start(f32[8,64,128]{2,1,0:T(8,128)} %get-tuple-element.13), channel_id=1, source_target_pairs={{0,2},{1,3},{2,4},{3,5},{4,6},{5,7},{6,8},{7,9},{8,10},{9,11},{10,... | collective-permute-start | bytes 786440 | tf_op jit(solution)/shard_map/ppermute | solution.py:88
  31.5 1.3 %collective-permute-start.2 = (f32[8,64,128]{2,1,0:T(8,128)}, f32[8,64,128]{2,1,0:T(8,128)S(1)}, u32[]{:S(2)}, u32[]{:S(2)}) collective-permute-start(f32[8,64,128]{2,1,0:T(8,128)} %get-tuple-element.14), channel_id=1, source_target_pairs={{2,0},{3,1},{4,2},{5,3},{6,4},{7,5},{8,6},{9,7},{10,8},{11,9},{12,... | collective-permute-start | bytes 786440 | tf_op jit(solution)/shard_map/ppermute | solution.py:88
  32.8 0.0 copy-start
  32.8 1.9 %copy-done = f32[32,64,384]{2,1,0:T(8,128)S(1)} copy-done((f32[32,64,384]{2,1,0:T(8,128)S(1)}, f32[32,64,384]{2,1,0:T(8,128)}, u32[]{:S(2)}) %copy-start) | copy-done | bytes 3145752
  34.6 0.0 copy-start.2
  34.6 1.2 %copy-done.2 = f32[2048,128]{1,0:T(8,128)S(1)} copy-done((f32[2048,128]{1,0:T(8,128)S(1)}, f32[2048,128]{1,0:T(8,128)}, u32[]{:S(2)}) %copy-start.2) | copy-done | bytes 1048600
  35.9 0.0 copy-start.3
  35.9 0.8 %copy-done.3 = f32[128,128]{1,0:T(8,128)S(1)} copy-done((f32[128,128]{1,0:T(8,128)S(1)}, f32[128,128]{1,0:T(8,128)}, u32[]{:S(2)}) %copy-start.3) | copy-done | bytes 65560
  36.7 0.0 copy-start.4
  36.7 0.7 copy-done.4
  37.4 0.0 copy-start.1
  37.4 9.8 %local_part.1 = (f32[32,64,128]{2,1,0:T(8,128)}, f32[24,64,128]{2,1,0:T(8,128)S(1)}, f32[8,128]{1,0:T(8,128)S(1)}) custom-call(s32[6,32]{1,0:T(8,128)S(1)} %bitcast.5, f32[32,64,128]{2,1,0:T(8,128)S(1)} %bitcast.4, f32[32,64,384]{2,1,0:T(8,128)S(1)} %copy-done, f32[128,128]{1,0:T(8,128)S(1)} %copy-done.3), custom_call_target="tpu_custom_call" | custom-call | tf_op jit(solution)/shard_map/local_part/pallas_call | solution.py:151
  47.2 0.0 collective-permute-done.rest_0_
  47.2 0.0 collective-permute-done.1.rest_1_
  47.2 0.0 collective-permute-done.2.rest_2_
  47.2 0.1 remote_quad.1
  47.3 13.3 %all_to_all.5.sums_ref = f32[16,1,128]{2,1,0:T(1,128)S(1)} all-to-all(f32[16,1,128]{2,1,0:T(1,128)S(1)} %remote_quad.1), channel_id=1, replica_groups=mesh['groups'=2,'space'=16] {'space'}, dimensions={0} | all-to-all | bytes 16384 | tf_op jit(solution)/shard_map/all_to_all | solution.py:296
  60.6 0.0 copy-done.5
  60.6 0.0 copy-done.1
  60.6 8.3 %remote_part.1 = (f32[32,64,128]{2,1,0:T(8,128)}, f32[1]{0:T(128)}) custom-call(s32[6,32]{1,0:T(8,128)S(1)} %bitcast.6, f32[128,128]{1,0:T(8,128)S(1)} %copy-done.3, f32[16,1,128]{2,1,0:T(1,128)S(1)} %all_to_all.5.sums_ref, f32[32,64,384]{2,1,0:T(8,128)S(1)} %copy-done.1, ...), custom_call_target="tpu_custom_call", output_to_operand_aliasing={{0}: (4, {})} | custom-call | tf_op jit(solution)/shard_map/remote_part/pallas_call | solution.py:261
Async XLA Ops:
  26.5 34.2 %copy-start.5 = (s32[32,6]{0,1:T(8,128)S(1)}, s32[32,6]{0,1:T(8,128)}, u32[]{:S(2)}) copy-start(s32[32,6]{0,1:T(8,128)} %param.9) | copy-start | bytes 2308
  26.5 20.7 %collective-permute-start = (f32[8,64,128]{2,1,0:T(8,128)}, f32[8,64,128]{2,1,0:T(8,128)S(1)}, u32[]{:S(2)}, u32[]{:S(2)}) collective-permute-start(f32[8,64,128]{2,1,0:T(8,128)} %get-tuple-element.12), channel_id=1, source_target_pairs={{0,1},{1,0},{2,3},{3,2},{4,5},{5,4},{6,7},{7,6},{8,9},{9,8},{10,11... | collective-permute-start | bytes 786440 | tf_op jit(solution)/shard_map/ppermute | solution.py:88
  27.0 20.2 %collective-permute-start.1 = (f32[8,64,128]{2,1,0:T(8,128)}, f32[8,64,128]{2,1,0:T(8,128)S(1)}, u32[]{:S(2)}, u32[]{:S(2)}) collective-permute-start(f32[8,64,128]{2,1,0:T(8,128)} %get-tuple-element.13), channel_id=1, source_target_pairs={{0,2},{1,3},{2,4},{3,5},{4,6},{5,7},{6,8},{7,9},{8,10},{9,11},{10,... | collective-permute-start | bytes 786440 | tf_op jit(solution)/shard_map/ppermute | solution.py:88
  31.5 15.8 %collective-permute-start.2 = (f32[8,64,128]{2,1,0:T(8,128)}, f32[8,64,128]{2,1,0:T(8,128)S(1)}, u32[]{:S(2)}, u32[]{:S(2)}) collective-permute-start(f32[8,64,128]{2,1,0:T(8,128)} %get-tuple-element.14), channel_id=1, source_target_pairs={{2,0},{3,1},{4,2},{5,3},{6,4},{7,5},{8,6},{9,7},{10,8},{11,9},{12,... | collective-permute-start | bytes 786440 | tf_op jit(solution)/shard_map/ppermute | solution.py:88
  32.8 1.9 %copy-start = (f32[32,64,384]{2,1,0:T(8,128)S(1)}, f32[32,64,384]{2,1,0:T(8,128)}, u32[]{:S(2)}) copy-start(f32[32,64,384]{2,1,0:T(8,128)} %a_hbm.1) | copy-start | bytes 9437188
  34.6 1.2 %copy-start.2 = (f32[2048,128]{1,0:T(8,128)S(1)}, f32[2048,128]{1,0:T(8,128)}, u32[]{:S(2)}) copy-start(f32[2048,128]{1,0:T(8,128)} %param.5) | copy-start | bytes 3145732
  35.9 0.8 %copy-start.3 = (f32[128,128]{1,0:T(8,128)S(1)}, f32[128,128]{1,0:T(8,128)}, u32[]{:S(2)}) copy-start(f32[128,128]{1,0:T(8,128)} %tree_ref.3) | copy-start | bytes 196612
  36.7 0.7 copy-start.4
  37.4 23.2 %copy-start.1 = (f32[32,64,384]{2,1,0:T(8,128)S(1)}, f32[32,64,384]{2,1,0:T(8,128)}, u32[]{:S(2)}) copy-start(f32[32,64,384]{2,1,0:T(8,128)} %a_hbm.1) | copy-start | bytes 9437188

commit v2 on v0

v2 whole, which is shorter than its diff:
```python
import math

import jax
import jax.numpy as jnp
from jax import lax
from jax.experimental import pallas as pl
from jax.experimental.pallas import tpu as pltpu
from jax.sharding import PartitionSpec as P

ROWS = 8
BLOCK = 4
HBM = pl.BlockSpec(memory_space=pltpu.HBM)
SMEM = pl.BlockSpec(memory_space=pltpu.SMEM)
VMEM = pl.BlockSpec(memory_space=pltpu.VMEM)
MIB = 1024 * 1024


def in_hbm(x):
    return pltpu.with_memory_space_constraint(x, pltpu.HBM)


def split(x):
    high = x.astype(jnp.bfloat16)
    return high, (x - high.astype(jnp.float32)).astype(jnp.bfloat16)


def stacked(x):
    return jnp.concatenate(split(x), axis=0)


def side_by_side(x):
    return jnp.concatenate(split(x), axis=1)


def dot(a, b, dims):
    return lax.dot_general(a, b, (dims, ((), ())), preferred_element_type=jnp.float32)


def quarters(s):
    rows, lanes = s.shape[0] // 2, s.shape[1] // 2
    return (s[rows:, lanes:] + s[rows:, :lanes]) + s[:rows, lanes:] + s[:rows, :lanes]


class Exchange:
    def __init__(self, count, cap):
        self.count, self.cap = count, cap
        self.wide = count // ROWS
        self.legs = [(self.wide, 0, 2, 3)]
        if ROWS > 2:
            self.legs.append((self.wide, 1, 2, 3))
        if self.wide > 1:
            self.legs.append((1, 0, 0, 1))
        if self.wide > 2:
            self.legs.append((1, 1, 0, 1))
        self.slots = len(self.legs) * cap

    def place(self, device, step):
        return device // self.wide if step == self.wide else device % self.wide

    def extent(self, step):
        return ROWS if step == self.wide else self.wide

    def route(self, leg):
        step, odd = leg[:2]
        pairs = []
        for i in range(self.count):
            at = self.place(i, step)
            if at % 2 == odd and at + 1 < self.extent(step):
                pairs += [(i, i + step), (i + step, i)]
        return pairs

    def sends(self, leg, device):
        step, odd, up, down = leg
        return jnp.where(self.place(device, step) % 2 == odd, up, down)

    def slot(self, column, own, device):
        entry = column - own
        direction = entry // self.cap
        base = jnp.int32(0)
        for i, leg in enumerate(self.legs):
            base = jnp.where(direction == leg[2] + leg[3] - self.sends(leg, device), i * self.cap, base)
        return jnp.where(entry < 0, self.slots, base + entry % self.cap)


def pick(lists, tiled, plan):
    cap, legs = plan.cap, plan.legs
    shape = pltpu.VMEM((cap,) + tiled.shape[1:], tiled.dtype)

    def kernel(lists_ref, tiled_ref, *rest):
        outs = rest[: len(legs)]
        numbers, sems, sem = rest[len(legs) :]
        device = lax.axis_index("space")
        load = pltpu.make_async_copy(lists_ref, numbers, sem)
        load.start()
        load.wait()
        copies = []
        for i, leg in enumerate(legs):
            direction = plan.sends(leg, device)
            for j in range(cap):
                tile = numbers[0, direction, j]
                copies.append(pltpu.make_async_copy(tiled_ref.at[tile], outs[i].at[j], sems.at[i, j]))
                copies[-1].start()
        for copy in copies:
            copy.wait()

    return pl.pallas_call(
        kernel,
        out_shape=[shape] * len(legs),
        in_specs=[HBM, HBM],
        out_specs=[VMEM] * len(legs),
        scratch_shapes=[
            pltpu.SMEM(lists.shape, jnp.int32),
            pltpu.SemaphoreType.DMA((len(legs), cap)),
            pltpu.SemaphoreType.DMA(()),
        ],
        compiler_params=pltpu.CompilerParams(vmem_limit_bytes=4 * MIB),
        name="pick",
    )(in_hbm(lists), in_hbm(tiled))


def local_part(columns, tiled, space_tiles, tree, plan):
    own, nodes, species = tiled.shape
    stored = columns.shape[0]
    slots = plan.slots
    block = BLOCK * nodes

    def kernel(columns_hbm, x_hbm, a_hbm, tree_hbm, product_hbm, p_ref, v_ref, quad_ref, meta_ref, *scratch):
        columns_ref, x_ref, a_ref, tree_ref, xs_ref, z_ref, c_sem, x_sem, a_sem, t_sem, sem = scratch
        device = lax.axis_index("space")

        def load(hbm, ref, sems, b):
            at = pl.ds(b * BLOCK, BLOCK)
            return pltpu.make_async_copy(hbm.at[at], ref.at[at], sems.at[b])

        load_columns = pltpu.make_async_copy(columns_hbm, columns_ref, c_sem)
        load_tree = pltpu.make_async_copy(tree_hbm, tree_ref, t_sem)
        for b in range(own // BLOCK):
            load(x_hbm, x_ref, x_sem, b).start()
        load_columns.start()
        load_tree.start()
        for b in range(own // BLOCK):
            load(a_hbm, a_ref, a_sem, b).start()
        xs_ref[own] = jnp.zeros((nodes, 2 * species), jnp.bfloat16)
        v_ref[...] = jnp.zeros(v_ref.shape, jnp.float32)
        for b in range(own // BLOCK):
            load(x_hbm, x_ref, x_sem, b).wait()
            c = b * BLOCK
            x = x_ref[c : c + BLOCK].reshape(block, species)
            xs_ref[c : c + BLOCK] = side_by_side(x).reshape(BLOCK, nodes, 2 * species)
        load_columns.wait()
        load_tree.wait()
        tree_rows = stacked(tree_ref[...])
        tree_lanes = side_by_side(tree_ref[...])

        def store(b):
            at = pl.ds(b * BLOCK, BLOCK)
            return pltpu.make_async_copy(p_ref.at[at], product_hbm.at[at], sem.at[b])

        def rows(b, carry):
            remote, quad = carry
            load(a_hbm, a_ref, a_sem, b).wait()
            parts = []
            for u in range(BLOCK):
                t = b * BLOCK + u
                tiles, last = [], jnp.int32(0)
                meta_ref[0, remote] = t
                for k in range(stored):
                    column = columns_ref[k, t]
                    last = jnp.maximum(last, column)
                    meta_ref[1 + k, remote] = plan.slot(column, own, device)
                    tiles.append(xs_ref[jnp.minimum(column, own)])
                remote = remote + (last >= own).astype(jnp.int32)
                parts.append(quarters(dot(stacked(a_ref[t]), jnp.concatenate(tiles, axis=0), ((1,), (0,)))))
            spatial = jnp.concatenate(parts, axis=0)
            at = pl.ds(b * BLOCK, BLOCK)
            xs = xs_ref[at].reshape(block, 2 * species)
            x = jnp.concatenate([xs[:, :species], xs[:, species:]], axis=0)
            z = quarters(dot(x, tree_lanes, ((1,), (0,))))
            z_ref[at] = z.reshape(BLOCK, nodes, species)
            product = quarters(dot(stacked(spatial), tree_rows, ((1,), (1,))))
            p_ref[at] = product.reshape(BLOCK, nodes, species)
            store(b).start()
            return remote, quad + (z * spatial).reshape(-1, 8, species).sum(axis=0)

        remote, quad = lax.fori_loop(0, own // BLOCK, rows, (jnp.int32(0), jnp.zeros((8, species), jnp.float32)))
        quad_ref[...] = quad
        blocks = (remote + BLOCK - 1) // BLOCK
        last_row = meta_ref[0, jnp.maximum(remote - 1, 0)]
        for u in range(BLOCK):
            meta_ref[0, remote + u] = last_row
            for k in range(stored):
                meta_ref[1 + k, remote + u] = slots
        meta_ref[1 + stored, 0] = remote

        def remote_rows(b, _):
            for u in range(BLOCK):
                i = b * BLOCK + u
                t = meta_ref[0, i]
                z = side_by_side(z_ref[t])
                w = dot(stacked(a_ref[t]), jnp.concatenate([z, z], axis=0), ((0,), (0,)))
                w = w[:, species:] + w[:, :species]
                for k in range(stored):
                    v_ref[meta_ref[1 + k, i]] += w[k * nodes : (k + 1) * nodes]
            return 0

        lax.fori_loop(0, blocks, remote_rows, 0)
        for b in range(own // BLOCK):
            store(b).wait()

    return pl.pallas_call(
        kernel,
        out_shape=[
            pltpu.HBM(tiled.shape, jnp.float32),
            pltpu.VMEM(tiled.shape, jnp.float32),
            pltpu.VMEM((slots + 1, nodes, species), jnp.float32),
            pltpu.VMEM((8, species), jnp.float32),
            pltpu.SMEM((stored + 2, own + BLOCK), jnp.int32),
        ],
        in_specs=[HBM] * 4,
        out_specs=[HBM, VMEM, VMEM, VMEM, SMEM],
        scratch_shapes=[
            pltpu.SMEM(columns.shape, jnp.int32),
            pltpu.VMEM(tiled.shape, jnp.float32),
            pltpu.VMEM(space_tiles.shape, jnp.float32),
            pltpu.VMEM(tree.shape, jnp.float32),
            pltpu.VMEM((own + 1, nodes, 2 * species), jnp.bfloat16),
            pltpu.VMEM(tiled.shape, jnp.float32),
            pltpu.SemaphoreType.DMA(()),
            pltpu.SemaphoreType.DMA((own // BLOCK,)),
            pltpu.SemaphoreType.DMA((own // BLOCK,)),
            pltpu.SemaphoreType.DMA(()),
            pltpu.SemaphoreType.DMA((own // BLOCK,)),
        ],
        compiler_params=pltpu.CompilerParams(vmem_limit_bytes=16 * MIB),
        name="local_part",
    )(in_hbm(columns), in_hbm(tiled), in_hbm(space_tiles), in_hbm(tree))


def remote_quad(v, quad, received, count):
    species = v.shape[2]
    cap = received[0].shape[0]

    def kernel(v_ref, quad_ref, *rest):
        parts, out_ref = rest[:-1], rest[-1]
        total = quad_ref[...]
        for i, part in enumerate(parts):
            for j in range(cap):
                total = total + (v_ref[i * cap + j] * part[j]).reshape(-1, 8, species).sum(axis=0)
        total = total.sum(axis=0, keepdims=True)
        for i in range(count):
            out_ref[i] = total

    return pl.pallas_call(
        kernel,
        out_shape=jax.ShapeDtypeStruct((count, 1, species), jnp.float32),
        in_specs=[VMEM] * (2 + len(received)),
        out_specs=VMEM,
        compiler_params=pltpu.CompilerParams(vmem_limit_bytes=8 * MIB),
        name="remote_quad",
    )(v, quad, *received)


def remote_part(meta, space_tiles, tree, local, product, received):
    own, nodes, species = product.shape
    stored = meta.shape[0] - 2
    legs, cap = len(received), received[0].shape[0]
    slots = legs * cap

    def kernel(meta_ref, tree_hbm, a_hbm, p_ref, *rest):
        parts = rest[:legs]
        _, out_hbm, tree_ref, a_ref, xs_ref, o_ref, t_sem, a_sem, sem = rest[legs:]
        remote = meta_ref[1 + stored, 0]
        padded = (remote + BLOCK - 1) // BLOCK * BLOCK

        def load(i):
            return pltpu.make_async_copy(a_hbm.at[meta_ref[0, i]], a_ref.at[i], a_sem.at[i])

        def begin(i, _):
            load(i).start()
            return 0

        load_tree = pltpu.make_async_copy(tree_hbm, tree_ref, t_sem)
        load_tree.start()
        lax.fori_loop(0, padded, begin, 0)
        xs_ref[slots] = jnp.zeros((nodes, 2 * species), jnp.bfloat16)
        for i in range(legs):
            x = parts[i][...].reshape(cap * nodes, species)
            xs_ref[i * cap : (i + 1) * cap] = side_by_side(x).reshape(cap, nodes, 2 * species)
        load_tree.wait()
        tree_rows = stacked(tree_ref[...])

        def store(i):
            return pltpu.make_async_copy(o_ref.at[i], out_hbm.at[meta_ref[0, i]], sem.at[i])

        def work(b, _):
            sums = []
            for u in range(BLOCK):
                i = b * BLOCK + u
                tiles = [xs_ref[meta_ref[1 + k, i]] for k in range(stored)]
                load(i).wait()
                a = stacked(a_ref[i])
                sums.append(quarters(dot(a, jnp.concatenate(tiles, axis=0), ((1,), (0,)))))
            added = quarters(dot(stacked(jnp.concatenate(sums, axis=0)), tree_rows, ((1,), (1,))))
            for u in range(BLOCK):
                i = b * BLOCK + u
                o_ref[i] = p_ref[meta_ref[0, i]] + added[u * nodes : (u + 1) * nodes]

                @pl.when(i < remote)
                def _():
                    store(i).start()

            return 0

        lax.fori_loop(0, padded // BLOCK, work, 0)

        def finish(i, _):
            store(i).wait()
            return 0

        lax.fori_loop(0, remote, finish, 0)

    return pl.pallas_call(
        kernel,
        out_shape=pltpu.HBM(product.shape, jnp.float32),
        in_specs=[SMEM, HBM, HBM] + [VMEM] * (1 + legs) + [HBM],
        out_specs=HBM,
        scratch_shapes=[
            pltpu.VMEM(tree.shape, jnp.float32),
            pltpu.VMEM((own + BLOCK,) + space_tiles.shape[1:], jnp.float32),
            pltpu.VMEM((slots + 1, nodes, 2 * species), jnp.bfloat16),
            pltpu.VMEM((own + BLOCK, nodes, species), jnp.float32),
            pltpu.SemaphoreType.DMA(()),
            pltpu.SemaphoreType.DMA((own + BLOCK,)),
            pltpu.SemaphoreType.DMA((own,)),
        ],
        input_output_aliases={4 + legs: 0},
        compiler_params=pltpu.CompilerParams(vmem_limit_bytes=16 * MIB),
        name="remote_part",
    )(meta, in_hbm(tree), in_hbm(space_tiles), local, *received, in_hbm(product))


def on_device(signal, space_tiles, tree_precision, send_tiles, column_tiles):
    count = lax.axis_size("space")
    tile_rows, tile_nodes = space_tiles.shape[:2]
    species = signal.shape[1]
    plan = Exchange(count, send_tiles.shape[2])
    tiled = signal.reshape(tile_rows, tile_nodes, species)
    outgoing = pick(send_tiles, tiled, plan)
    received = [lax.ppermute(o, "space", plan.route(leg)) for o, leg in zip(outgoing, plan.legs)]
    product, local, v, quad, meta = local_part(column_tiles.T, tiled, space_tiles, tree_precision, plan)
    shares = remote_quad(v, quad, received, count)
    sums = lax.all_to_all(shares, "space", 0, 0)
    product = remote_part(meta, space_tiles, tree_precision, local, product, received)
    scale = 1.0 / math.sqrt(count * tile_rows * tile_nodes * species)
    return product.reshape(signal.shape), (jnp.sum(sums) * scale).reshape(1)


def solution(mesh):
    placed = (
        P(("groups", "space"), None),
        P("space", None, None),
        P("groups", None),
        P("space", None, None),
        P("space", None),
    )
    return jax.shard_map(
        on_device,
        mesh=mesh,
        in_specs=placed,
        out_specs=(P(("groups", "space"), None), P("groups")),
        check_vma=False,
    )
```

time: 83.4 us -> 32.7 us (0.39)
  blocking collectives: 34.3 us -> 0 us
  local copies, waits for them, and re-layouts: 23.8 us -> 0 us
  Pallas kernels: 0 us -> 15.5 us
  matrix products: 9.46 us -> 0 us
  waiting for transfers between devices: 0.01 us -> 4 us
  starting transfers between devices: 11.8 us -> 9.74 us
    psum x1 -> x0, blocking collectives: 34.3 us -> none  [on_device(): total = lax.psum(jnp.sum(signal * product), 'space')]
    pallas_call x0 -> x4, Pallas kernels: none -> 15.5 us  [the longest x1 8.58 us: local_part(): pl.pallas_call(kernel, out_shape=[pltpu.HBM(tiled.shape, jnp.float32), pl...]
    gather x5 -> x0, local copies, waits for them, and re-layouts: 14.6 us -> none  [the longest x4 9.36 us: receive_lists(): outgoing = tiled[lists[direction]]]
    dot_general x2 -> x0, matrix products: 9.46 us -> none  [the longest x1 6.84 us: on_device(): jnp.einsum('rac,rcs->ras', space_tiles, gathered, precision=lax.Precision...]
    ppermute x4 -> x3, starting transfers between devices: 11.8 us -> 3.77 us  [on_device(): lax.ppermute(o, 'space', plan.route(leg))]
    unnamed x12 -> x0, local copies, waits for them, and re-layouts: 7.37 us -> none
    all_to_all x0 -> x1, starting transfers between devices: none -> 5.97 us  [on_device(): sums = lax.all_to_all(shares, 'space', 0, 0)]
    all_to_all x0 -> x1, waiting for transfers between devices: none -> 2.16 us  [on_device(): sums = lax.all_to_all(shares, 'space', 0, 0)]
  transfers between devices with their start and end apart: 4 -> 4, of which waited for: 0 -> 2; matrix products, arithmetic and copies ran while one was open for 18% -> 0% of each run, Pallas kernels for 0% -> 40%
where the time goes in v2:
time: 32.7 us; the launch traced here: 32.3 us
  Pallas kernels  15.5 us (47%)
  starting transfers between devices  9.74 us (30%)
  waiting for transfers between devices  4 us (12%)
  between operations  2.46 us (8%)
  other arithmetic  0.62 us (2%)
    pallas_call x1, Pallas kernels, local_part(): pl.pallas_call(kernel, out_shape=[pltpu.HBM(tiled.shape, jnp.float32), pl...  8.58 us
    all_to_all x1, starting transfers between devices, on_device(): sums = lax.all_to_all(shares, 'space', 0, 0)  5.97 us
    pallas_call x1, Pallas kernels, remote_part(): pl.pallas_call(kernel, out_shape=pltpu.HBM(product.shape, jnp.float32), i...  4.23 us
    ppermute x3, starting transfers between devices, on_device(): lax.ppermute(o, 'space', plan.route(leg))  3.77 us
    all_to_all x1, waiting for transfers between devices, on_device(): sums = lax.all_to_all(shares, 'space', 0, 0)  2.16 us
    pallas_call x1, Pallas kernels, pick(): pl.pallas_call(kernel, out_shape=[shape] * len(legs), in_specs=[HBM, HBM]...  2.01 us
    ppermute x3, waiting for transfers between devices, on_device(): lax.ppermute(o, 'space', plan.route(leg))  1.84 us
    pallas_call x1, Pallas kernels, remote_quad(): pl.pallas_call(kernel, out_shape=jax.ShapeDtypeStruct((count, 1, species)...  0.68 us
  transfers between devices with their start and end apart: 4, of which 2 were waited for; matrix products, arithmetic and copies ran while one was open for 0% of the time, Pallas kernels for 40%

profile of v2, /device:TPU:0, one launch (start us, length us, event | category | flops | bytes accessed | tf_op | source)
XLA Modules:
  0.0 32.3 jit_solution(4910533434135819931)
XLA Ops:
  0.6 2.0 %pick.1 = (f32[8,64,128]{2,1,0:T(8,128)S(1)}, f32[8,64,128]{2,1,0:T(8,128)S(1)}, f32[8,64,128]{2,1,0:T(8,128)S(1)}) custom-call(s32[1,4,8]{2,1,0:T(4,128)} %lists_ref.1, f32[32,64,128]{2,1,0:T(8,128)} %bitcast.4), custom_call_target="tpu_custom_call" | custom-call | tf_op jit(solution)/shard_map/pick/pallas_call | solution.py:106
  2.7 3.0 %collective-permute-start = (f32[8,64,128]{2,1,0:T(8,128)S(1)}, f32[8,64,128]{2,1,0:T(8,128)S(1)}, u32[]{:S(2)}, u32[]{:S(2)}) collective-permute-start(f32[8,64,128]{2,1,0:T(8,128)S(1)} %get-tuple-element.12), channel_id=1, source_target_pairs={{0,2},{2,0},{1,3},{3,1},{4,6},{6,4},{5,7},{7,5},{8,10},{10,8},{9,1... | collective-permute-start | bytes 786440 | tf_op jit(solution)/shard_map/ppermute | solution.py:349
  5.7 0.7 %collective-permute-start.1 = (f32[8,64,128]{2,1,0:T(8,128)S(1)}, f32[8,64,128]{2,1,0:T(8,128)S(1)}, u32[]{:S(2)}, u32[]{:S(2)}) collective-permute-start(f32[8,64,128]{2,1,0:T(8,128)S(1)} %get-tuple-element.13), channel_id=1, source_target_pairs={{2,4},{4,2},{3,5},{5,3},{6,8},{8,6},{7,9},{9,7},{10,12},{12,10},{1... | collective-permute-start | bytes 786440 | tf_op jit(solution)/shard_map/ppermute | solution.py:349
  6.4 0.1 collective-permute-start.2
  6.4 8.6 %local_part.1 = (f32[32,64,128]{2,1,0:T(8,128)}, f32[32,64,128]{2,1,0:T(8,128)S(1)}, f32[25,64,128]{2,1,0:T(8,128)S(1)}, f32[8,128]{1,0:T(8,128)S(1)}, s32[8,36]{1,0:T(8,128)S(4)}) custom-call(s32[6,32]{1,0:T(8,128)} %bitcast.7, f32[32,64,128]{2,1,0:T(8,128)} %bitcast.5, f32[32,64,384]{2,1,0:T(8,128)} %a_hbm.3, f32[128,128]{1,0:T(8,128)} %tree_hbm.3), custom_call_target="tpu_custom_call" | custom-call | tf_op jit(solution)/shard_map/local_part/pallas_call | solution.py:210
  15.0 1.8 %collective-permute-done.rest_0_ = f32[8,64,128]{2,1,0:T(8,128)S(1)} collective-permute-done((f32[8,64,128]{2,1,0:T(8,128)S(1)}, f32[8,64,128]{2,1,0:T(8,128)S(1)}, u32[]{:S(2)}, u32[]{:S(2)}) %collective-permute-start) | collective-permute-done | bytes 262176 | tf_op jit(solution)/shard_map/ppermute | solution.py:349
  16.9 0.0 collective-permute-done.1.rest_1_
  16.9 0.0 collective-permute-done.2.rest_2_
  16.9 0.7 %remote_quad.1 = f32[16,1,128]{2,1,0:T(1,128)} custom-call(f32[25,64,128]{2,1,0:T(8,128)S(1)} %get-tuple-element.16.v_ref, f32[8,128]{1,0:T(8,128)S(1)} %get-tuple-element.17.quad_ref, f32[8,64,128]{2,1,0:T(8,128)S(1)} %collective-permute-done.rest_0_, f32[8,64,128]{2,1,0:T(8,128)S(1)} %collective-permute-done.1.rest_1_, ...), custom_call_target="tpu_custom_call" | custom-call | tf_op jit(solution)/shard_map/remote_quad/pallas_call | solution.py:253
  17.6 6.0 %all-to-all-start = ((f32[16,1,128]{2,1,0:T(1,128)}), f32[16,1,128]{2,1,0:T(1,128)S(1)}, u32[]{:S(2)}, u32[]{:S(2)}) async-start(f32[16,1,128]{2,1,0:T(1,128)} %remote_quad.1), calls=%async_computation | async-start | bytes 16384 | tf_op jit(solution)/shard_map/all_to_all | solution.py:352
  23.5 4.2 %remote_part.1 = f32[32,64,128]{2,1,0:T(8,128)} custom-call(s32[8,36]{1,0:T(8,128)S(4)} %get-tuple-element.10.meta_ref, f32[128,128]{1,0:T(8,128)} %tree_hbm.3, f32[32,64,384]{2,1,0:T(8,128)} %a_hbm.3, f32[32,64,128]{2,1,0:T(8,128)S(1)} %get-tuple-element.11.p_ref, f32[8,64,128]{2,1,0:T(8,128)S(1)} %collective-permute-done.rest_0_, ...), custom_call_target="tpu_custom_call", output_to_operand_aliasing={{}: (7, {})} | custom-call | tf_op jit(solution)/shard_map/remote_part/pallas_call | solution.py:322
  27.8 2.2 %all-to-all-done = f32[16,1,128]{2,1,0:T(1,128)S(1)} async-done(((f32[16,1,128]{2,1,0:T(1,128)}), f32[16,1,128]{2,1,0:T(1,128)S(1)}, u32[]{:S(2)}, u32[]{:S(2)}) %all-to-all-start) | async-done | bytes 8224 | tf_op jit(solution)/shard_map/all_to_all | solution.py:352
  29.9 0.6 %reduce_sum.9 = f32[]{:T(128)} reduce(f32[16,1,128]{2,1,0:T(1,128)S(1)} %all-to-all-done, f32[]{:T(128)} %constant.0.clone.1), dimensions={0,1,2}, to_apply=%region_0.0 | reduce | flops 2047 | bytes 8200 | tf_op jit(solution)/shard_map/reduce_sum | solution.py:355
Async XLA Ops:
  2.7 14.2 %collective-permute-start = (f32[8,64,128]{2,1,0:T(8,128)S(1)}, f32[8,64,128]{2,1,0:T(8,128)S(1)}, u32[]{:S(2)}, u32[]{:S(2)}) collective-permute-start(f32[8,64,128]{2,1,0:T(8,128)S(1)} %get-tuple-element.12), channel_id=1, source_target_pairs={{0,2},{2,0},{1,3},{3,1},{4,6},{6,4},{5,7},{7,5},{8,10},{10,8},{9,1... | collective-permute-start | bytes 786440 | tf_op jit(solution)/shard_map/ppermute | solution.py:349
  5.7 11.2 %collective-permute-start.1 = (f32[8,64,128]{2,1,0:T(8,128)S(1)}, f32[8,64,128]{2,1,0:T(8,128)S(1)}, u32[]{:S(2)}, u32[]{:S(2)}) collective-permute-start(f32[8,64,128]{2,1,0:T(8,128)S(1)} %get-tuple-element.13), channel_id=1, source_target_pairs={{2,4},{4,2},{3,5},{5,3},{6,8},{8,6},{7,9},{9,7},{10,12},{12,10},{1... | collective-permute-start | bytes 786440 | tf_op jit(solution)/shard_map/ppermute | solution.py:349
  6.4 10.5 %collective-permute-start.2 = (f32[8,64,128]{2,1,0:T(8,128)S(1)}, f32[8,64,128]{2,1,0:T(8,128)S(1)}, u32[]{:S(2)}, u32[]{:S(2)}) collective-permute-start(f32[8,64,128]{2,1,0:T(8,128)S(1)} %get-tuple-element.14), channel_id=1, source_target_pairs={{0,1},{1,0},{2,3},{3,2},{4,5},{5,4},{6,7},{7,6},{8,9},{9,8},{10,11... | collective-permute-start | bytes 786440 | tf_op jit(solution)/shard_map/ppermute | solution.py:349
  17.6 12.4 %all-to-all-start = ((f32[16,1,128]{2,1,0:T(1,128)}), f32[16,1,128]{2,1,0:T(1,128)S(1)}, u32[]{:S(2)}, u32[]{:S(2)}) async-start(f32[16,1,128]{2,1,0:T(1,128)} %remote_quad.1), calls=%async_computation | async-start | bytes 16384 | tf_op jit(solution)/shard_map/all_to_all | solution.py:352

commit v3 on v2

--- a/solution.py
+++ b/solution.py
@@ -8,6 +8,7 @@
 from jax.sharding import PartitionSpec as P
 
 ROWS = 8
+LOCAL_BLOCK = 8
 BLOCK = 4
 HBM = pl.BlockSpec(memory_space=pltpu.HBM)
 SMEM = pl.BlockSpec(memory_space=pltpu.SMEM)
@@ -39,6 +40,21 @@
 def quarters(s):
     rows, lanes = s.shape[0] // 2, s.shape[1] // 2
     return (s[rows:, lanes:] + s[rows:, :lanes]) + s[:rows, lanes:] + s[:rows, :lanes]
+
+
+def halves(s):
+    lanes = s.shape[1] // 2
+    return s[:, lanes:] + s[:, :lanes]
+
+
+def tree_forward(tree):
+    rows = stacked(tree)
+    return jnp.concatenate([rows, rows], axis=1)
+
+
+def tree_backward(tree):
+    lanes = side_by_side(tree)
+    return jnp.concatenate([lanes, lanes], axis=0)
 
 
 class Exchange:
@@ -84,33 +100,35 @@
 
 def pick(lists, tiled, plan):
     cap, legs = plan.cap, plan.legs
+    chunks = 4
+    chunk = tiled.shape[0] // chunks
     shape = pltpu.VMEM((cap,) + tiled.shape[1:], tiled.dtype)
 
-    def kernel(lists_ref, tiled_ref, *rest):
-        outs = rest[: len(legs)]
-        numbers, sems, sem = rest[len(legs) :]
+    def kernel(lists_hbm, tiled_hbm, *rest):
+        outs, tiled_ref = rest[: len(legs)], rest[len(legs)]
+        lists_ref, sems, sem = rest[len(legs) + 1 :]
+        loads = [pltpu.make_async_copy(lists_hbm, lists_ref, sem)]
+        for i in range(chunks):
+            at = pl.ds(i * chunk, chunk)
+            loads.append(pltpu.make_async_copy(tiled_hbm.at[at], tiled_ref.at[at], sems.at[i]))
+        for load in loads:
+            load.start()
         device = lax.axis_index("space")
-        load = pltpu.make_async_copy(lists_ref, numbers, sem)
-        load.start()
-        load.wait()
-        copies = []
-        for i, leg in enumerate(legs):
-            direction = plan.sends(leg, device)
+        directions = [plan.sends(leg, device) for leg in legs]
+        for load in loads:
+            load.wait()
+        for i, direction in enumerate(directions):
             for j in range(cap):
-                tile = numbers[0, direction, j]
-                copies.append(pltpu.make_async_copy(tiled_ref.at[tile], outs[i].at[j], sems.at[i, j]))
-                copies[-1].start()
-        for copy in copies:
-            copy.wait()
+                outs[i][j] = tiled_ref[lists_ref[0, direction, j]]
 
     return pl.pallas_call(
         kernel,
-        out_shape=[shape] * len(legs),
+        out_shape=[shape] * len(legs) + [pltpu.VMEM(tiled.shape, tiled.dtype)],
         in_specs=[HBM, HBM],
-        out_specs=[VMEM] * len(legs),
+        out_specs=[VMEM] * (len(legs) + 1),
         scratch_shapes=[
             pltpu.SMEM(lists.shape, jnp.int32),
-            pltpu.SemaphoreType.DMA((len(legs), cap)),
+            pltpu.SemaphoreType.DMA((chunks,)),
             pltpu.SemaphoreType.DMA(()),
         ],
         compiler_params=pltpu.CompilerParams(vmem_limit_bytes=4 * MIB),
@@ -122,89 +140,90 @@
     own, nodes, species = tiled.shape
     stored = columns.shape[0]
     slots = plan.slots
-    block = BLOCK * nodes
-
-    def kernel(columns_hbm, x_hbm, a_hbm, tree_hbm, product_hbm, p_ref, v_ref, quad_ref, meta_ref, *scratch):
-        columns_ref, x_ref, a_ref, tree_ref, xs_ref, z_ref, c_sem, x_sem, a_sem, t_sem, sem = scratch
+    blocks = own // LOCAL_BLOCK
+    block = LOCAL_BLOCK * nodes
+
+    def kernel(columns_hbm, x_ref, a_hbm, tree_hbm, product_hbm, p_ref, v_ref, quad_ref, meta_ref, *scratch):
+        columns_ref, a_ref, tree_ref, xs_ref, c_sem, a_sem, t_sem, p_sem = scratch
         device = lax.axis_index("space")
 
         def load(hbm, ref, sems, b):
-            at = pl.ds(b * BLOCK, BLOCK)
+            at = pl.ds(b * LOCAL_BLOCK, LOCAL_BLOCK)
             return pltpu.make_async_copy(hbm.at[at], ref.at[at], sems.at[b])
+
+        def store(b):
+            return load(p_ref, product_hbm, p_sem, b)
 
         load_columns = pltpu.make_async_copy(columns_hbm, columns_ref, c_sem)
         load_tree = pltpu.make_async_copy(tree_hbm, tree_ref, t_sem)
-        for b in range(own // BLOCK):
-            load(x_hbm, x_ref, x_sem, b).start()
         load_columns.start()
         load_tree.start()
-        for b in range(own // BLOCK):
+        for b in range(blocks):
             load(a_hbm, a_ref, a_sem, b).start()
+
+        def clear(i, _):
+            v_ref[i] = jnp.zeros((nodes, species), jnp.float32)
+            return 0
+
+        lax.fori_loop(0, slots + 1, clear, 0)
         xs_ref[own] = jnp.zeros((nodes, 2 * species), jnp.bfloat16)
-        v_ref[...] = jnp.zeros(v_ref.shape, jnp.float32)
-        for b in range(own // BLOCK):
-            load(x_hbm, x_ref, x_sem, b).wait()
-            c = b * BLOCK
-            x = x_ref[c : c + BLOCK].reshape(block, species)
-            xs_ref[c : c + BLOCK] = side_by_side(x).reshape(BLOCK, nodes, 2 * species)
+
+        def prepare(b, _):
+            at = pl.ds(b * LOCAL_BLOCK, LOCAL_BLOCK)
+            xs_ref[at] = side_by_side(x_ref[at].reshape(block, species)).reshape(LOCAL_BLOCK, nodes, 2 * species)
+            return 0
+
+        lax.fori_loop(0, blocks, prepare, 0)
         load_columns.wait()
         load_tree.wait()
-        tree_rows = stacked(tree_ref[...])
-        tree_lanes = side_by_side(tree_ref[...])
-
-        def store(b):
-            at = pl.ds(b * BLOCK, BLOCK)
-            return pltpu.make_async_copy(p_ref.at[at], product_hbm.at[at], sem.at[b])
+        forward = tree_forward(tree_ref[...])
 
         def rows(b, carry):
             remote, quad = carry
             load(a_hbm, a_ref, a_sem, b).wait()
             parts = []
-            for u in range(BLOCK):
-                t = b * BLOCK + u
+            for u in range(LOCAL_BLOCK):
+                t = b * LOCAL_BLOCK + u
                 tiles, last = [], jnp.int32(0)
-                meta_ref[0, remote] = t
                 for k in range(stored):
                     column = columns_ref[k, t]
                     last = jnp.maximum(last, column)
-                    meta_ref[1 + k, remote] = plan.slot(column, own, device)
                     tiles.append(xs_ref[jnp.minimum(column, own)])
+                meta_ref[0, remote] = t
                 remote = remote + (last >= own).astype(jnp.int32)
                 parts.append(quarters(dot(stacked(a_ref[t]), jnp.concatenate(tiles, axis=0), ((1,), (0,)))))
-            spatial = jnp.concatenate(parts, axis=0)
-            at = pl.ds(b * BLOCK, BLOCK)
-            xs = xs_ref[at].reshape(block, 2 * species)
-            x = jnp.concatenate([xs[:, :species], xs[:, species:]], axis=0)
-            z = quarters(dot(x, tree_lanes, ((1,), (0,))))
-            z_ref[at] = z.reshape(BLOCK, nodes, species)
-            product = quarters(dot(stacked(spatial), tree_rows, ((1,), (1,))))
-            p_ref[at] = product.reshape(BLOCK, nodes, species)
+            product = halves(dot(side_by_side(jnp.concatenate(parts, axis=0)), forward, ((1,), (1,))))
+            at = pl.ds(b * LOCAL_BLOCK, LOCAL_BLOCK)
+            p_ref[at] = product.reshape(LOCAL_BLOCK, nodes, species)
             store(b).start()
-            return remote, quad + (z * spatial).reshape(-1, 8, species).sum(axis=0)
-
-        remote, quad = lax.fori_loop(0, own // BLOCK, rows, (jnp.int32(0), jnp.zeros((8, species), jnp.float32)))
+            x = x_ref[at].reshape(block, species)
+            return remote, quad + (x * product).reshape(-1, 8, species).sum(axis=0)
+
+        remote, quad = lax.fori_loop(0, blocks, rows, (jnp.int32(0), jnp.zeros((8, species), jnp.float32)))
         quad_ref[...] = quad
-        blocks = (remote + BLOCK - 1) // BLOCK
         last_row = meta_ref[0, jnp.maximum(remote - 1, 0)]
         for u in range(BLOCK):
             meta_ref[0, remote + u] = last_row
-            for k in range(stored):
-                meta_ref[1 + k, remote + u] = slots
         meta_ref[1 + stored, 0] = remote
+        backward = tree_backward(tree_ref[...])
 
         def remote_rows(b, _):
-            for u in range(BLOCK):
+            rows = [meta_ref[0, b * BLOCK + u] for u in range(BLOCK)]
+            x = jnp.concatenate([xs_ref[t] for t in rows], axis=0)
+            z = side_by_side(halves(dot(x, backward, ((1,), (0,)))))
+            for u, t in enumerate(rows):
                 i = b * BLOCK + u
-                t = meta_ref[0, i]
-                z = side_by_side(z_ref[t])
-                w = dot(stacked(a_ref[t]), jnp.concatenate([z, z], axis=0), ((0,), (0,)))
-                w = w[:, species:] + w[:, :species]
+                mine = z[u * nodes : (u + 1) * nodes]
+                w = halves(dot(stacked(a_ref[t]), jnp.concatenate([mine, mine], axis=0), ((0,), (0,))))
                 for k in range(stored):
-                    v_ref[meta_ref[1 + k, i]] += w[k * nodes : (k + 1) * nodes]
-            return 0
-
-        lax.fori_loop(0, blocks, remote_rows, 0)
-        for b in range(own // BLOCK):
+                    slot = plan.slot(columns_ref[k, t], own, device)
+                    slot = jnp.where(i < remote, slot, slots)
+                    meta_ref[1 + k, i] = slot
+                    v_ref[slot] += w[k * nodes : (k + 1) * nodes]
+            return 0
+
+        lax.fori_loop(0, (remote + BLOCK - 1) // BLOCK, remote_rows, 0)
+        for b in range(blocks):
             store(b).wait()
 
     return pl.pallas_call(
@@ -216,24 +235,21 @@
             pltpu.VMEM((8, species), jnp.float32),
             pltpu.SMEM((stored + 2, own + BLOCK), jnp.int32),
         ],
-        in_specs=[HBM] * 4,
+        in_specs=[HBM, VMEM, HBM, HBM],
         out_specs=[HBM, VMEM, VMEM, VMEM, SMEM],
         scratch_shapes=[
             pltpu.SMEM(columns.shape, jnp.int32),
-            pltpu.VMEM(tiled.shape, jnp.float32),
             pltpu.VMEM(space_tiles.shape, jnp.float32),
             pltpu.VMEM(tree.shape, jnp.float32),
             pltpu.VMEM((own + 1, nodes, 2 * species), jnp.bfloat16),
-            pltpu.VMEM(tiled.shape, jnp.float32),
             pltpu.SemaphoreType.DMA(()),
-            pltpu.SemaphoreType.DMA((own // BLOCK,)),
-            pltpu.SemaphoreType.DMA((own // BLOCK,)),
+            pltpu.SemaphoreType.DMA((blocks,)),
             pltpu.SemaphoreType.DMA(()),
-            pltpu.SemaphoreType.DMA((own // BLOCK,)),
+            pltpu.SemaphoreType.DMA((blocks,)),
         ],
         compiler_params=pltpu.CompilerParams(vmem_limit_bytes=16 * MIB),
         name="local_part",
-    )(in_hbm(columns), in_hbm(tiled), in_hbm(space_tiles), in_hbm(tree))
+    )(in_hbm(columns), tiled, in_hbm(space_tiles), in_hbm(tree))
 
 
 def remote_quad(v, quad, received, count):
@@ -252,7 +268,7 @@
 
     return pl.pallas_call(
         kernel,
-        out_shape=jax.ShapeDtypeStruct((count, 1, species), jnp.float32),
+        out_shape=pltpu.VMEM((count, 1, species), jnp.float32),
         in_specs=[VMEM] * (2 + len(received)),
         out_specs=VMEM,
         compiler_params=pltpu.CompilerParams(vmem_limit_bytes=8 * MIB),
@@ -287,7 +303,7 @@
             x = parts[i][...].reshape(cap * nodes, species)
             xs_ref[i * cap : (i + 1) * cap] = side_by_side(x).reshape(cap, nodes, 2 * species)
         load_tree.wait()
-        tree_rows = stacked(tree_ref[...])
+        forward = tree_forward(tree_ref[...])
 
         def store(i):
             return pltpu.make_async_copy(o_ref.at[i], out_hbm.at[meta_ref[0, i]], sem.at[i])
@@ -300,7 +316,7 @@
                 load(i).wait()
                 a = stacked(a_ref[i])
                 sums.append(quarters(dot(a, jnp.concatenate(tiles, axis=0), ((1,), (0,)))))
-            added = quarters(dot(stacked(jnp.concatenate(sums, axis=0)), tree_rows, ((1,), (1,))))
+            added = halves(dot(side_by_side(jnp.concatenate(sums, axis=0)), forward, ((1,), (1,))))
             for u in range(BLOCK):
                 i = b * BLOCK + u
                 o_ref[i] = p_ref[meta_ref[0, i]] + added[u * nodes : (u + 1) * nodes]
@@ -345,7 +361,7 @@
     species = signal.shape[1]
     plan = Exchange(count, send_tiles.shape[2])
     tiled = signal.reshape(tile_rows, tile_nodes, species)
-    outgoing = pick(send_tiles, tiled, plan)
+    *outgoing, tiled = pick(send_tiles, tiled, plan)
     received = [lax.ppermute(o, "space", plan.route(leg)) for o, leg in zip(outgoing, plan.legs)]
     product, local, v, quad, meta = local_part(column_tiles.T, tiled, space_tiles, tree_precision, plan)
     shares = remote_quad(v, quad, received, count)

time: 32.7 us -> 31.8 us (0.972)
  Pallas kernels: 15.5 us -> 11.4 us
  waiting for transfers between devices: 4 us -> 7.42 us
    ppermute x3, waiting for transfers between devices: 1.84 us -> 5.15 us  [on_device(): lax.ppermute(o, 'space', plan.route(leg))]
    pallas_call x1, Pallas kernels: 8.58 us -> 5.27 us  [local_part(): pl.pallas_call(kernel, out_shape=[pltpu.HBM(tiled.shape, jnp.float32), pl...]
    pallas_call x2, Pallas kernels: 2.7 us -> 1.97 us  [the longest x1 1.28 us: pick(): pl.pallas_call(kernel, out_shape=[shape] * len(legs) + [pltpu.VMEM(tiled....]
  transfers between devices with their start and end apart: 4 -> 4, of which waited for: 2 -> 2; matrix products, arithmetic and copies ran while one was open for 0% -> 0% of each run, Pallas kernels for 40% -> 30%
where the time goes in v3:
time: 31.8 us; the launch traced here: 31.6 us
  Pallas kernels  11.4 us (36%)
  starting transfers between devices  9.71 us (31%)
  waiting for transfers between devices  7.42 us (23%)
  between operations  2.46 us (8%)
  other arithmetic  0.62 us (2%)
    all_to_all x1, starting transfers between devices, on_device(): sums = lax.all_to_all(shares, 'space', 0, 0)  5.94 us
    pallas_call x1, Pallas kernels, local_part(): pl.pallas_call(kernel, out_shape=[pltpu.HBM(tiled.shape, jnp.float32), pl...  5.27 us
    ppermute x3, waiting for transfers between devices, on_device(): lax.ppermute(o, 'space', plan.route(leg))  5.15 us
    pallas_call x1, Pallas kernels, remote_part(): pl.pallas_call(kernel, out_shape=pltpu.HBM(product.shape, jnp.float32), i...  4.13 us
    ppermute x3, starting transfers between devices, on_device(): lax.ppermute(o, 'space', plan.route(leg))  3.77 us
    all_to_all x1, waiting for transfers between devices, on_device(): sums = lax.all_to_all(shares, 'space', 0, 0)  2.26 us
    pallas_call x1, Pallas kernels, pick(): pl.pallas_call(kernel, out_shape=[shape] * len(legs) + [pltpu.VMEM(tiled....  1.28 us
    pallas_call x1, Pallas kernels, remote_quad(): pl.pallas_call(kernel, out_shape=pltpu.VMEM((count, 1, species), jnp.floa...  0.68 us
  transfers between devices with their start and end apart: 4, of which 2 were waited for; matrix products, arithmetic and copies ran while one was open for 0% of the time, Pallas kernels for 30%

profile of v3, /device:TPU:0, one launch (start us, length us, event | category | flops | bytes accessed | tf_op | source)
XLA Modules:
  0.0 31.6 jit_solution(577316877827973267)
XLA Ops:
  0.6 1.3 %pick.1 = (f32[8,64,128]{2,1,0:T(8,128)S(1)}, f32[8,64,128]{2,1,0:T(8,128)S(1)}, f32[8,64,128]{2,1,0:T(8,128)S(1)}, f32[32,64,128]{2,1,0:T(8,128)S(1)}) custom-call(s32[1,4,8]{2,1,0:T(4,128)} %lists_hbm.1, f32[32,64,128]{2,1,0:T(8,128)} %bitcast.5), custom_call_target="tpu_custom_call" | custom-call | tf_op jit(solution)/shard_map/pick/pallas_call | solution.py:124
  1.9 3.0 %collective-permute-start = (f32[8,64,128]{2,1,0:T(8,128)S(1)}, f32[8,64,128]{2,1,0:T(8,128)S(1)}, u32[]{:S(2)}, u32[]{:S(2)}) collective-permute-start(f32[8,64,128]{2,1,0:T(8,128)S(1)} %get-tuple-element.14), channel_id=1, source_target_pairs={{0,2},{2,0},{1,3},{3,1},{4,6},{6,4},{5,7},{7,5},{8,10},{10,8},{9,1... | collective-permute-start | bytes 786440 | tf_op jit(solution)/shard_map/ppermute | solution.py:365
  5.0 0.7 %collective-permute-start.1 = (f32[8,64,128]{2,1,0:T(8,128)S(1)}, f32[8,64,128]{2,1,0:T(8,128)S(1)}, u32[]{:S(2)}, u32[]{:S(2)}) collective-permute-start(f32[8,64,128]{2,1,0:T(8,128)S(1)} %get-tuple-element.15), channel_id=1, source_target_pairs={{2,4},{4,2},{3,5},{5,3},{6,8},{8,6},{7,9},{9,7},{10,12},{12,10},{1... | collective-permute-start | bytes 786440 | tf_op jit(solution)/shard_map/ppermute | solution.py:365
  5.6 0.1 collective-permute-start.2
  5.7 5.3 %local_part.1 = (f32[32,64,128]{2,1,0:T(8,128)}, f32[32,64,128]{2,1,0:T(8,128)S(1)}, f32[25,64,128]{2,1,0:T(8,128)S(1)}, f32[8,128]{1,0:T(8,128)S(1)}, s32[8,36]{1,0:T(8,128)S(4)}) custom-call(s32[6,32]{1,0:T(8,128)} %bitcast.6, f32[32,64,128]{2,1,0:T(8,128)S(1)} %get-tuple-element.11.x_ref, f32[32,64,384]{2,1,0:T(8,128)} %a_hbm.3, f32[128,128]{1,0:T(8,128)} %tree_hbm.3), custom_call_target="tpu_custom_call" | custom-call | tf_op jit(solution)/shard_map/local_part/pallas_call | solution.py:229
  11.0 5.1 %collective-permute-done.rest_0_ = f32[8,64,128]{2,1,0:T(8,128)S(1)} collective-permute-done((f32[8,64,128]{2,1,0:T(8,128)S(1)}, f32[8,64,128]{2,1,0:T(8,128)S(1)}, u32[]{:S(2)}, u32[]{:S(2)}) %collective-permute-start) | collective-permute-done | bytes 262176 | tf_op jit(solution)/shard_map/ppermute | solution.py:365
  16.1 0.0 collective-permute-done.1.rest_1_
  16.1 0.0 collective-permute-done.2.rest_2_
  16.1 0.7 %remote_quad.1 = f32[16,1,128]{2,1,0:T(1,128)} custom-call(f32[25,64,128]{2,1,0:T(8,128)S(1)} %get-tuple-element.18.v_ref, f32[8,128]{1,0:T(8,128)S(1)} %get-tuple-element.19.quad_ref, f32[8,64,128]{2,1,0:T(8,128)S(1)} %collective-permute-done.rest_0_, f32[8,64,128]{2,1,0:T(8,128)S(1)} %collective-permute-done.1.rest_1_, ...), custom_call_target="tpu_custom_call" | custom-call | tf_op jit(solution)/shard_map/remote_quad/pallas_call | solution.py:269
  16.8 5.9 %all-to-all-start = ((f32[16,1,128]{2,1,0:T(1,128)}), f32[16,1,128]{2,1,0:T(1,128)S(1)}, u32[]{:S(2)}, u32[]{:S(2)}) async-start(f32[16,1,128]{2,1,0:T(1,128)} %remote_quad.1), calls=%async_computation | async-start | bytes 16384 | tf_op jit(solution)/shard_map/all_to_all | solution.py:368
  22.8 4.1 %remote_part.1 = f32[32,64,128]{2,1,0:T(8,128)} custom-call(s32[8,36]{1,0:T(8,128)S(4)} %get-tuple-element.12.meta_ref, f32[128,128]{1,0:T(8,128)} %tree_hbm.3, f32[32,64,384]{2,1,0:T(8,128)} %a_hbm.3, f32[32,64,128]{2,1,0:T(8,128)S(1)} %get-tuple-element.13.p_ref, f32[8,64,128]{2,1,0:T(8,128)S(1)} %collective-permute-done.rest_0_, ...), custom_call_target="tpu_custom_call", output_to_operand_aliasing={{}: (7, {})} | custom-call | tf_op jit(solution)/shard_map/remote_part/pallas_call | solution.py:338
  26.9 2.3 %all-to-all-done = f32[16,1,128]{2,1,0:T(1,128)S(1)} async-done(((f32[16,1,128]{2,1,0:T(1,128)}), f32[16,1,128]{2,1,0:T(1,128)S(1)}, u32[]{:S(2)}, u32[]{:S(2)}) %all-to-all-start) | async-done | bytes 8224 | tf_op jit(solution)/shard_map/all_to_all | solution.py:368
  29.2 0.6 %reduce_sum.9 = f32[]{:T(128)} reduce(f32[16,1,128]{2,1,0:T(1,128)S(1)} %all-to-all-done, f32[]{:T(128)} %constant.0.clone.1), dimensions={0,1,2}, to_apply=%region_0.0 | reduce | flops 2047 | bytes 8200 | tf_op jit(solution)/shard_map/reduce_sum | solution.py:371
Async XLA Ops:
  1.9 14.2 %collective-permute-start = (f32[8,64,128]{2,1,0:T(8,128)S(1)}, f32[8,64,128]{2,1,0:T(8,128)S(1)}, u32[]{:S(2)}, u32[]{:S(2)}) collective-permute-start(f32[8,64,128]{2,1,0:T(8,128)S(1)} %get-tuple-element.14), channel_id=1, source_target_pairs={{0,2},{2,0},{1,3},{3,1},{4,6},{6,4},{5,7},{7,5},{8,10},{10,8},{9,1... | collective-permute-start | bytes 786440 | tf_op jit(solution)/shard_map/ppermute | solution.py:365
  5.0 11.2 %collective-permute-start.1 = (f32[8,64,128]{2,1,0:T(8,128)S(1)}, f32[8,64,128]{2,1,0:T(8,128)S(1)}, u32[]{:S(2)}, u32[]{:S(2)}) collective-permute-start(f32[8,64,128]{2,1,0:T(8,128)S(1)} %get-tuple-element.15), channel_id=1, source_target_pairs={{2,4},{4,2},{3,5},{5,3},{6,8},{8,6},{7,9},{9,7},{10,12},{12,10},{1... | collective-permute-start | bytes 786440 | tf_op jit(solution)/shard_map/ppermute | solution.py:365
  5.6 10.5 %collective-permute-start.2 = (f32[8,64,128]{2,1,0:T(8,128)S(1)}, f32[8,64,128]{2,1,0:T(8,128)S(1)}, u32[]{:S(2)}, u32[]{:S(2)}) collective-permute-start(f32[8,64,128]{2,1,0:T(8,128)S(1)} %get-tuple-element.16), channel_id=1, source_target_pairs={{0,1},{1,0},{2,3},{3,2},{4,5},{5,4},{6,7},{7,6},{8,9},{9,8},{10,11... | collective-permute-start | bytes 786440 | tf_op jit(solution)/shard_map/ppermute | solution.py:365
  16.8 12.3 %all-to-all-start = ((f32[16,1,128]{2,1,0:T(1,128)}), f32[16,1,128]{2,1,0:T(1,128)S(1)}, u32[]{:S(2)}, u32[]{:S(2)}) async-start(f32[16,1,128]{2,1,0:T(1,128)} %remote_quad.1), calls=%async_computation | async-start | bytes 16384 | tf_op jit(solution)/shard_map/all_to_all | solution.py:368

commit v4 on v3

--- a/solution.py
+++ b/solution.py
@@ -143,8 +143,9 @@
     blocks = own // LOCAL_BLOCK
     block = LOCAL_BLOCK * nodes
 
-    def kernel(columns_hbm, x_ref, a_hbm, tree_hbm, product_hbm, p_ref, v_ref, quad_ref, meta_ref, *scratch):
-        columns_ref, a_ref, tree_ref, xs_ref, c_sem, a_sem, t_sem, p_sem = scratch
+    def kernel(columns_hbm, x_ref, a_hbm, tree_hbm, product_hbm, *rest):
+        p_ref, v_ref, quad_ref, meta_ref, forward_ref, a_ref = rest[:6]
+        columns_ref, tree_ref, xs_ref, c_sem, a_sem, t_sem, p_sem = rest[6:]
         device = lax.axis_index("space")
 
         def load(hbm, ref, sems, b):
@@ -177,6 +178,7 @@
         load_columns.wait()
         load_tree.wait()
         forward = tree_forward(tree_ref[...])
+        forward_ref[...] = forward
 
         def rows(b, carry):
             remote, quad = carry
@@ -234,12 +236,13 @@
             pltpu.VMEM((slots + 1, nodes, species), jnp.float32),
             pltpu.VMEM((8, species), jnp.float32),
             pltpu.SMEM((stored + 2, own + BLOCK), jnp.int32),
+            pltpu.VMEM((2 * species, 2 * species), jnp.bfloat16),
+            pltpu.VMEM(space_tiles.shape, jnp.float32),
         ],
         in_specs=[HBM, VMEM, HBM, HBM],
-        out_specs=[HBM, VMEM, VMEM, VMEM, SMEM],
+        out_specs=[HBM, VMEM, VMEM, VMEM, SMEM, VMEM, VMEM],
         scratch_shapes=[
             pltpu.SMEM(columns.shape, jnp.int32),
-            pltpu.VMEM(space_tiles.shape, jnp.float32),
             pltpu.VMEM(tree.shape, jnp.float32),
             pltpu.VMEM((own + 1, nodes, 2 * species), jnp.bfloat16),
             pltpu.SemaphoreType.DMA(()),
@@ -252,7 +255,7 @@
     )(in_hbm(columns), tiled, in_hbm(space_tiles), in_hbm(tree))
 
 
-def remote_quad(v, quad, received, count):
+def remote_quad(v, quad, received):
     species = v.shape[2]
     cap = received[0].shape[0]
 
@@ -262,13 +265,11 @@
         for i, part in enumerate(parts):
             for j in range(cap):
                 total = total + (v_ref[i * cap + j] * part[j]).reshape(-1, 8, species).sum(axis=0)
-        total = total.sum(axis=0, keepdims=True)
-        for i in range(count):
-            out_ref[i] = total
-
-    return pl.pallas_call(
-        kernel,
-        out_shape=pltpu.VMEM((count, 1, species), jnp.float32),
+        out_ref[...] = total.sum(axis=0, keepdims=True)
+
+    return pl.pallas_call(
+        kernel,
+        out_shape=pltpu.VMEM((1, species), jnp.float32),
         in_specs=[VMEM] * (2 + len(received)),
         out_specs=VMEM,
         compiler_params=pltpu.CompilerParams(vmem_limit_bytes=8 * MIB),
@@ -276,83 +277,111 @@
     )(v, quad, *received)
 
 
-def remote_part(meta, space_tiles, tree, local, product, received):
-    own, nodes, species = product.shape
+def swap_rounds(count):
+    masks = [1 << bit for bit in range(count.bit_length() - 1)]
+    if 1 << len(masks) != count or len(masks) < 4:
+        return []
+    return [masks[-1:], [1, 2, 3]] + [[mask] for mask in masks[-2:1:-1]]
+
+
+def swap_sum(x, count, beside):
+    rounds = swap_rounds(count)
+    if not rounds:
+        return lax.psum(x, "space"), jnp.zeros_like(x), beside
+    for i, masks in enumerate(rounds):
+        others = [lax.ppermute(x, "space", [(j, j ^ mask) for j in range(count)]) for mask in masks]
+        if i == len(rounds) - 1:
+            return x, others[0], beside
+        x = x + others[0]
+        if len(others) == 3:
+            x = x + (others[1] + others[2])
+        if i == 0:
+            x, beside = lax.optimization_barrier((x, beside))
+
+
+def remote_part(meta, space_tiles, forward, local, received):
+    own, nodes, species = local.shape
     stored = meta.shape[0] - 2
     legs, cap = len(received), received[0].shape[0]
     slots = legs * cap
 
-    def kernel(meta_ref, tree_hbm, a_hbm, p_ref, *rest):
-        parts = rest[:legs]
-        _, out_hbm, tree_ref, a_ref, xs_ref, o_ref, t_sem, a_sem, sem = rest[legs:]
-        remote = meta_ref[1 + stored, 0]
-        padded = (remote + BLOCK - 1) // BLOCK * BLOCK
-
-        def load(i):
-            return pltpu.make_async_copy(a_hbm.at[meta_ref[0, i]], a_ref.at[i], a_sem.at[i])
-
-        def begin(i, _):
-            load(i).start()
-            return 0
-
-        load_tree = pltpu.make_async_copy(tree_hbm, tree_ref, t_sem)
-        load_tree.start()
-        lax.fori_loop(0, padded, begin, 0)
+    def kernel(meta_ref, forward_ref, a_ref, p_ref, *rest):
+        parts, (o_ref, xs_ref) = rest[:legs], rest[legs:]
         xs_ref[slots] = jnp.zeros((nodes, 2 * species), jnp.bfloat16)
         for i in range(legs):
             x = parts[i][...].reshape(cap * nodes, species)
             xs_ref[i * cap : (i + 1) * cap] = side_by_side(x).reshape(cap, nodes, 2 * species)
-        load_tree.wait()
-        forward = tree_forward(tree_ref[...])
-
-        def store(i):
-            return pltpu.make_async_copy(o_ref.at[i], out_hbm.at[meta_ref[0, i]], sem.at[i])
+        forward = forward_ref[...]
 
         def work(b, _):
+            rows = [meta_ref[0, b * BLOCK + u] for u in range(BLOCK)]
             sums = []
-            for u in range(BLOCK):
-                i = b * BLOCK + u
-                tiles = [xs_ref[meta_ref[1 + k, i]] for k in range(stored)]
-                load(i).wait()
-                a = stacked(a_ref[i])
-                sums.append(quarters(dot(a, jnp.concatenate(tiles, axis=0), ((1,), (0,)))))
+            for u, t in enumerate(rows):
+                tiles = [xs_ref[meta_ref[1 + k, b * BLOCK + u]] for k in range(stored)]
+                sums.append(quarters(dot(stacked(a_ref[t]), jnp.concatenate(tiles, axis=0), ((1,), (0,)))))
             added = halves(dot(side_by_side(jnp.concatenate(sums, axis=0)), forward, ((1,), (1,))))
-            for u in range(BLOCK):
-                i = b * BLOCK + u
-                o_ref[i] = p_ref[meta_ref[0, i]] + added[u * nodes : (u + 1) * nodes]
-
-                @pl.when(i < remote)
-                def _():
-                    store(i).start()
-
-            return 0
-
-        lax.fori_loop(0, padded // BLOCK, work, 0)
-
-        def finish(i, _):
-            store(i).wait()
-            return 0
-
-        lax.fori_loop(0, remote, finish, 0)
-
-    return pl.pallas_call(
-        kernel,
-        out_shape=pltpu.HBM(product.shape, jnp.float32),
-        in_specs=[SMEM, HBM, HBM] + [VMEM] * (1 + legs) + [HBM],
-        out_specs=HBM,
-        scratch_shapes=[
-            pltpu.VMEM(tree.shape, jnp.float32),
-            pltpu.VMEM((own + BLOCK,) + space_tiles.shape[1:], jnp.float32),
-            pltpu.VMEM((slots + 1, nodes, 2 * species), jnp.bfloat16),
-            pltpu.VMEM((own + BLOCK, nodes, species), jnp.float32),
-            pltpu.SemaphoreType.DMA(()),
-            pltpu.SemaphoreType.DMA((own + BLOCK,)),
-            pltpu.SemaphoreType.DMA((own,)),
-        ],
-        input_output_aliases={4 + legs: 0},
+            for u, t in enumerate(rows):
+                o_ref[b * BLOCK + u] = p_ref[t] + added[u * nodes : (u + 1) * nodes]
+            return 0
+
+        lax.fori_loop(0, (meta_ref[1 + stored, 0] + BLOCK - 1) // BLOCK, work, 0)
+
+    return pl.pallas_call(
+        kernel,
+        out_shape=pltpu.VMEM((own + BLOCK, nodes, species), jnp.float32),
+        in_specs=[SMEM] + [VMEM] * (3 + legs),
+        out_specs=VMEM,
+        scratch_shapes=[pltpu.VMEM((slots + 1, nodes, 2 * species), jnp.bfloat16)],
         compiler_params=pltpu.CompilerParams(vmem_limit_bytes=16 * MIB),
         name="remote_part",
-    )(meta, in_hbm(tree), in_hbm(space_tiles), local, *received, in_hbm(product))
+    )(meta, forward, space_tiles, local, *received)
+
+
+def store(meta, changed, product):
+    own = product.shape[0]
+    stored = meta.shape[0] - 2
+
+    def kernel(meta_ref, changed_ref, _, product_hbm, sems):
+        remote = meta_ref[1 + stored, 0]
+
+        def copy(i):
+            return pltpu.make_async_copy(changed_ref.at[i], product_hbm.at[meta_ref[0, i]], sems.at[i])
+
+        def begin(i, _):
+            copy(i).start()
+            return 0
+
+        def end(i, _):
+            copy(i).wait()
+            return 0
+
+        lax.fori_loop(0, remote, begin, 0)
+        lax.fori_loop(0, remote, end, 0)
+
+    return pl.pallas_call(
+        kernel,
+        out_shape=pltpu.HBM(product.shape, jnp.float32),
+        in_specs=[SMEM, VMEM, HBM],
+        out_specs=HBM,
+        scratch_shapes=[pltpu.SemaphoreType.DMA((own,))],
+        input_output_aliases={2: 0},
+        compiler_params=pltpu.CompilerParams(vmem_limit_bytes=8 * MIB),
+        name="store",
+    )(meta, changed, in_hbm(product))
+
+
+def finish(x, y, scale):
+    def kernel(x_ref, y_ref, quad_ref):
+        quad_ref[0] = jnp.sum(x_ref[...] + y_ref[...]) * scale
+
+    return pl.pallas_call(
+        kernel,
+        out_shape=jax.ShapeDtypeStruct((1,), jnp.float32),
+        in_specs=[VMEM, VMEM],
+        out_specs=SMEM,
+        compiler_params=pltpu.CompilerParams(vmem_limit_bytes=MIB),
+        name="finish",
+    )(x, y)
 
 
 def on_device(signal, space_tiles, tree_precision, send_tiles, column_tiles):
@@ -363,12 +392,15 @@
     tiled = signal.reshape(tile_rows, tile_nodes, species)
     *outgoing, tiled = pick(send_tiles, tiled, plan)
     received = [lax.ppermute(o, "space", plan.route(leg)) for o, leg in zip(outgoing, plan.legs)]
-    product, local, v, quad, meta = local_part(column_tiles.T, tiled, space_tiles, tree_precision, plan)
-    shares = remote_quad(v, quad, received, count)
-    sums = lax.all_to_all(shares, "space", 0, 0)
-    product = remote_part(meta, space_tiles, tree_precision, local, product, received)
+    product, local, v, quad, meta, forward, space_tiles = local_part(
+        column_tiles.T, tiled, space_tiles, tree_precision, plan
+    )
+    share = remote_quad(v, quad, received)
+    changed = remote_part(meta, space_tiles, forward, local, received)
+    x, y, changed = swap_sum(share, count, changed)
+    product = store(meta, changed, product)
     scale = 1.0 / math.sqrt(count * tile_rows * tile_nodes * species)
-    return product.reshape(signal.shape), (jnp.sum(sums) * scale).reshape(1)
+    return product.reshape(signal.shape), finish(x, y, scale)
 
 
 def solution(mesh):

time: 31.8 us -> 29.4 us (0.925)
  Pallas kernels: 11.4 us -> 9.28 us
  between operations: 2.46 us -> 0.69 us
  starting transfers between devices: 9.71 us -> 11.3 us
  other arithmetic: 0.62 us -> 0.01 us
  waiting for transfers between devices: 7.42 us -> 7.91 us
    ppermute x0 -> x5, starting transfers between devices: none -> 7.56 us  [swap_sum(): lax.ppermute(x, 'space', [(j, j ^ mask) for j in range(count)])]
    all_to_all x1 -> x0, starting transfers between devices: 5.94 us -> none  [on_device(): sums = lax.all_to_all(shares, 'space', 0, 0)]
    ppermute x0 -> x5, waiting for transfers between devices: none -> 2.75 us  [swap_sum(): lax.ppermute(x, 'space', [(j, j ^ mask) for j in range(count)])]
    all_to_all x1 -> x0, waiting for transfers between devices: 2.26 us -> none  [on_device(): sums = lax.all_to_all(shares, 'space', 0, 0)]
    pallas_call x2 -> x4, Pallas kernels: 4.81 us -> 2.73 us  [the longest x1 1.02 us: remote_part(): pl.pallas_call(kernel, out_shape=pltpu.VMEM((own + BLOCK, nodes, species)...]
    reduce_sum x1 -> x0, other arithmetic: 0.62 us -> none  [on_device(): return (product.reshape(signal.shape), (jnp.sum(sums) * scale).reshape(1))]
  transfers between devices with their start and end apart: 4 -> 8, of which waited for: 2 -> 5; matrix products, arithmetic and copies ran while one was open for 0% -> 0% of each run, Pallas kernels for 30% -> 25%
where the time goes in v4:
time: 29.4 us; the launch traced here: 29.2 us
  starting transfers between devices  11.3 us (38%)
  Pallas kernels  9.28 us (32%)
  waiting for transfers between devices  7.91 us (27%)
  between operations  0.69 us (2%)
    ppermute x5, starting transfers between devices, swap_sum(): lax.ppermute(x, 'space', [(j, j ^ mask) for j in range(count)])  7.56 us
    pallas_call x1, Pallas kernels, local_part(): pl.pallas_call(kernel, out_shape=[pltpu.HBM(tiled.shape, jnp.float32), pl...  5.27 us
    ppermute x3, waiting for transfers between devices, on_device(): lax.ppermute(o, 'space', plan.route(leg))  5.16 us
    ppermute x3, starting transfers between devices, on_device(): lax.ppermute(o, 'space', plan.route(leg))  3.77 us
    ppermute x5, waiting for transfers between devices, swap_sum(): lax.ppermute(x, 'space', [(j, j ^ mask) for j in range(count)])  2.75 us
    pallas_call x1, Pallas kernels, pick(): pl.pallas_call(kernel, out_shape=[shape] * len(legs) + [pltpu.VMEM(tiled....  1.28 us
    pallas_call x1, Pallas kernels, remote_part(): pl.pallas_call(kernel, out_shape=pltpu.VMEM((own + BLOCK, nodes, species)...  1.02 us
    pallas_call x1, Pallas kernels, store(): pl.pallas_call(kernel, out_shape=pltpu.HBM(product.shape, jnp.float32), i...  0.97 us
  transfers between devices with their start and end apart: 8, of which 5 were waited for; matrix products, arithmetic and copies ran while one was open for 0% of the time, Pallas kernels for 25%

profile of v4, /device:TPU:0, one launch (start us, length us, event | category | flops | bytes accessed | tf_op | source)
XLA Modules:
  0.0 29.2 jit_solution(12322683046795640509)
XLA Ops:
  0.6 1.3 %pick.1 = (f32[8,64,128]{2,1,0:T(8,128)S(1)}, f32[8,64,128]{2,1,0:T(8,128)S(1)}, f32[8,64,128]{2,1,0:T(8,128)S(1)}, f32[32,64,128]{2,1,0:T(8,128)S(1)}) custom-call(s32[1,4,8]{2,1,0:T(4,128)} %lists_hbm.1, f32[32,64,128]{2,1,0:T(8,128)} %bitcast.3), custom_call_target="tpu_custom_call" | custom-call | tf_op jit(solution)/shard_map/pick/pallas_call | solution.py:124
  1.9 3.0 %collective-permute-start = (f32[8,64,128]{2,1,0:T(8,128)S(1)}, f32[8,64,128]{2,1,0:T(8,128)S(1)}, u32[]{:S(2)}, u32[]{:S(2)}) collective-permute-start(f32[8,64,128]{2,1,0:T(8,128)S(1)} %get-tuple-element.19), channel_id=1, source_target_pairs={{0,2},{2,0},{1,3},{3,1},{4,6},{6,4},{5,7},{7,5},{8,10},{10,8},{9,1... | collective-permute-start | bytes 786440 | tf_op jit(solution)/shard_map/ppermute | solution.py:394
  5.0 0.7 %collective-permute-start.1 = (f32[8,64,128]{2,1,0:T(8,128)S(1)}, f32[8,64,128]{2,1,0:T(8,128)S(1)}, u32[]{:S(2)}, u32[]{:S(2)}) collective-permute-start(f32[8,64,128]{2,1,0:T(8,128)S(1)} %get-tuple-element.20), channel_id=1, source_target_pairs={{2,4},{4,2},{3,5},{5,3},{6,8},{8,6},{7,9},{9,7},{10,12},{12,10},{1... | collective-permute-start | bytes 786440 | tf_op jit(solution)/shard_map/ppermute | solution.py:394
  5.6 0.1 collective-permute-start.2
  5.7 5.3 %local_part.1 = (f32[32,64,128]{2,1,0:T(8,128)}, f32[32,64,128]{2,1,0:T(8,128)S(1)}, f32[25,64,128]{2,1,0:T(8,128)S(1)}, f32[8,128]{1,0:T(8,128)S(1)}, s32[8,36]...) custom-call(s32[6,32]{1,0:T(8,128)} %bitcast.5, f32[32,64,128]{2,1,0:T(8,128)S(1)} %get-tuple-element.15.x_ref, ...), custom_call_target="tpu_custom_call" | custom-call | tf_op jit(solution)/shard_map/local_part/pallas_call | solution.py:231
  11.0 5.2 %collective-permute-done.rest_0_ = f32[8,64,128]{2,1,0:T(8,128)S(1)} collective-permute-done((f32[8,64,128]{2,1,0:T(8,128)S(1)}, f32[8,64,128]{2,1,0:T(8,128)S(1)}, u32[]{:S(2)}, u32[]{:S(2)}) %collective-permute-start) | collective-permute-done | bytes 262176 | tf_op jit(solution)/shard_map/ppermute | solution.py:394
  16.1 0.0 collective-permute-done.1.rest_1_
  16.1 0.0 collective-permute-done.2.rest_2_
  16.1 0.1 remote_quad.1
  16.2 3.6 %collective-permute-start.3 = (f32[1,128]{1,0:T(1,128)S(1)}, f32[1,128]{1,0:T(1,128)S(1)}, u32[]{:S(2)}, u32[]{:S(2)}) collective-permute-start(f32[1,128]{1,0:T(1,128)S(1)} %remote_quad.1), channel_id=1, source_target_pairs={{0,8},{1,9},{2,10},{3,11},{4,12},{5,13},{6,14},{7,15},{8,0},{9,1},... | collective-permute-start | bytes 1544 | tf_op jit(solution)/shard_map/ppermute | solution.py:292
  19.9 1.0 %remote_part.1.changed_ref = f32[36,64,128]{2,1,0:T(8,128)S(1)} custom-call(s32[8,36]{1,0:T(8,128)S(4)} %get-tuple-element.16.meta_ref, bf16[256,256]{1,0:T(8,128)(2,1)S(1)} %get-tuple-element.22.forward_ref, f32[32,64,384]{2,1,0:T(8,128)S(1)} %get-tuple-element.23.a_ref, f32[32,64,128]{2,1,0:T(8,128)S(1)} %get-tuple-element.24.p_ref, ...), custom_call_target="tpu_custom_call" | custom-call | tf_op jit(solution)/shard_map/remote_part/pallas_call | solution.py:329
  20.9 0.5 %collective-permute-done.3 = f32[1,128]{1,0:T(1,128)S(1)} collective-permute-done((f32[1,128]{1,0:T(1,128)S(1)}, f32[1,128]{1,0:T(1,128)S(1)}, u32[]{:S(2)}, u32[]{:S(2)}) %collective-permute-start.3) | collective-permute-done | bytes 544 | tf_op jit(solution)/shard_map/ppermute | solution.py:292
  21.4 0.0 collective-permute-start.6
  21.4 1.9 %collective-permute-start.5 = (f32[1,128]{1,0:T(1,128)S(1)}, f32[1,128]{1,0:T(1,128)S(1)}, u32[]{:S(2)}, u32[]{:S(2)}) collective-permute-start(f32[1,128]{1,0:T(1,128)S(1)} %add.12), channel_id=1, source_target_pairs={{0,2},{1,3},{2,0},{3,1},{4,6},{5,7},{6,4},{7,5},{8,10},{9,11},{10,... | collective-permute-start | bytes 1544 | tf_op jit(solution)/shard_map/ppermute | solution.py:292
  23.3 0.1 collective-permute-start.4
  23.4 1.0 %collective-permute-done.6 = f32[1,128]{1,0:T(1,128)S(1)} collective-permute-done((f32[1,128]{1,0:T(1,128)S(1)}, f32[1,128]{1,0:T(1,128)S(1)}, u32[]{:S(2)}, u32[]{:S(2)}) %collective-permute-start.6) | collective-permute-done | bytes 544 | tf_op jit(solution)/shard_map/ppermute | solution.py:292
  24.4 0.6 %collective-permute-done.5 = f32[1,128]{1,0:T(1,128)S(1)} collective-permute-done((f32[1,128]{1,0:T(1,128)S(1)}, f32[1,128]{1,0:T(1,128)S(1)}, u32[]{:S(2)}, u32[]{:S(2)}) %collective-permute-start.5) | collective-permute-done | bytes 544 | tf_op jit(solution)/shard_map/ppermute | solution.py:292
  25.0 0.0 collective-permute-done.4
  25.0 2.0 %collective-permute-start.7 = (f32[1,128]{1,0:T(1,128)S(1)}, f32[1,128]{1,0:T(1,128)S(1)}, u32[]{:S(2)}, u32[]{:S(2)}) collective-permute-start(f32[1,128]{1,0:T(1,128)S(1)} %add_add_fusion.x_ref), channel_id=1, source_target_pairs={{0,4},{1,5},{2,6},{3,7},{4,0},{5,1},{6,2},{7,3},{8,12},{9,13},{10,... | collective-permute-start | bytes 1544 | tf_op jit(solution)/shard_map/ppermute | solution.py:292
  26.9 1.0 %store.1 = f32[32,64,128]{2,1,0:T(8,128)} custom-call(s32[8,36]{1,0:T(8,128)S(4)} %get-tuple-element.16.meta_ref, f32[36,64,128]{2,1,0:T(8,128)S(1)} %remote_part.1.changed_ref, f32[32,64,128]{2,1,0:T(8,128)} %get-tuple-element.26._), custom_call_target="tpu_custom_call", output_to_operand_aliasing={{}: (2, {})} | custom-call | tf_op jit(solution)/shard_map/store/pallas_call | solution.py:361
  27.9 0.7 %collective-permute-done.7.y_ref = f32[1,128]{1,0:T(1,128)S(1)} collective-permute-done((f32[1,128]{1,0:T(1,128)S(1)}, f32[1,128]{1,0:T(1,128)S(1)}, u32[]{:S(2)}, u32[]{:S(2)}) %collective-permute-start.7) | collective-permute-done | bytes 544 | tf_op jit(solution)/shard_map/ppermute | solution.py:292
  28.6 0.6 %finish.1 = f32[1]{0:T(128)} custom-call(f32[1,128]{1,0:T(1,128)S(1)} %add_add_fusion.x_ref, f32[1,128]{1,0:T(1,128)S(1)} %collective-permute-done.7.y_ref), custom_call_target="tpu_custom_call" | custom-call | tf_op jit(solution)/shard_map/finish/pallas_call | solution.py:377
  (2 shorter events, 0.0 us)
Async XLA Ops:
  1.9 14.2 %collective-permute-start = (f32[8,64,128]{2,1,0:T(8,128)S(1)}, f32[8,64,128]{2,1,0:T(8,128)S(1)}, u32[]{:S(2)}, u32[]{:S(2)}) collective-permute-start(f32[8,64,128]{2,1,0:T(8,128)S(1)} %get-tuple-element.19), channel_id=1, source_target_pairs={{0,2},{2,0},{1,3},{3,1},{4,6},{6,4},{5,7},{7,5},{8,10},{10,8},{9,1... | collective-permute-start | bytes 786440 | tf_op jit(solution)/shard_map/ppermute | solution.py:394
  5.0 11.2 %collective-permute-start.1 = (f32[8,64,128]{2,1,0:T(8,128)S(1)}, f32[8,64,128]{2,1,0:T(8,128)S(1)}, u32[]{:S(2)}, u32[]{:S(2)}) collective-permute-start(f32[8,64,128]{2,1,0:T(8,128)S(1)} %get-tuple-element.20), channel_id=1, source_target_pairs={{2,4},{4,2},{3,5},{5,3},{6,8},{8,6},{7,9},{9,7},{10,12},{12,10},{1... | collective-permute-start | bytes 786440 | tf_op jit(solution)/shard_map/ppermute | solution.py:394
  5.6 10.5 %collective-permute-start.2 = (f32[8,64,128]{2,1,0:T(8,128)S(1)}, f32[8,64,128]{2,1,0:T(8,128)S(1)}, u32[]{:S(2)}, u32[]{:S(2)}) collective-permute-start(f32[8,64,128]{2,1,0:T(8,128)S(1)} %get-tuple-element.21), channel_id=1, source_target_pairs={{0,1},{1,0},{2,3},{3,2},{4,5},{5,4},{6,7},{7,6},{8,9},{9,8},{10,11... | collective-permute-start | bytes 786440 | tf_op jit(solution)/shard_map/ppermute | solution.py:394
  16.2 5.1 %collective-permute-start.3 = (f32[1,128]{1,0:T(1,128)S(1)}, f32[1,128]{1,0:T(1,128)S(1)}, u32[]{:S(2)}, u32[]{:S(2)}) collective-permute-start(f32[1,128]{1,0:T(1,128)S(1)} %remote_quad.1), channel_id=1, source_target_pairs={{0,8},{1,9},{2,10},{3,11},{4,12},{5,13},{6,14},{7,15},{8,0},{9,1},... | collective-permute-start | bytes 1544 | tf_op jit(solution)/shard_map/ppermute | solution.py:292
  21.4 3.0 %collective-permute-start.6 = (f32[1,128]{1,0:T(1,128)S(1)}, f32[1,128]{1,0:T(1,128)S(1)}, u32[]{:S(2)}, u32[]{:S(2)}) collective-permute-start(f32[1,128]{1,0:T(1,128)S(1)} %add.12), channel_id=1, source_target_pairs={{0,3},{1,2},{2,1},{3,0},{4,7},{5,6},{6,5},{7,4},{8,11},{9,10},{10,... | collective-permute-start | bytes 1544 | tf_op jit(solution)/shard_map/ppermute | solution.py:292
  21.4 3.6 %collective-permute-start.5 = (f32[1,128]{1,0:T(1,128)S(1)}, f32[1,128]{1,0:T(1,128)S(1)}, u32[]{:S(2)}, u32[]{:S(2)}) collective-permute-start(f32[1,128]{1,0:T(1,128)S(1)} %add.12), channel_id=1, source_target_pairs={{0,2},{1,3},{2,0},{3,1},{4,6},{5,7},{6,4},{7,5},{8,10},{9,11},{10,... | collective-permute-start | bytes 1544 | tf_op jit(solution)/shard_map/ppermute | solution.py:292
  23.3 1.7 %collective-permute-start.4 = (f32[1,128]{1,0:T(1,128)S(1)}, f32[1,128]{1,0:T(1,128)S(1)}, u32[]{:S(2)}, u32[]{:S(2)}) collective-permute-start(f32[1,128]{1,0:T(1,128)S(1)} %add.12), channel_id=1, source_target_pairs={{0,1},{1,0},{2,3},{3,2},{4,5},{5,4},{6,7},{7,6},{8,9},{9,8},{10,11... | collective-permute-start | bytes 1544 | tf_op jit(solution)/shard_map/ppermute | solution.py:292
  25.0 3.6 %collective-permute-start.7 = (f32[1,128]{1,0:T(1,128)S(1)}, f32[1,128]{1,0:T(1,128)S(1)}, u32[]{:S(2)}, u32[]{:S(2)}) collective-permute-start(f32[1,128]{1,0:T(1,128)S(1)} %add_add_fusion.x_ref), channel_id=1, source_target_pairs={{0,4},{1,5},{2,6},{3,7},{4,0},{5,1},{6,2},{7,3},{8,12},{9,13},{10,... | collective-permute-start | bytes 1544 | tf_op jit(solution)/shard_map/ppermute | solution.py:292

commit v5 on v4

--- a/solution.py
+++ b/solution.py
@@ -277,26 +277,24 @@
     )(v, quad, *received)
 
 
-def swap_rounds(count):
+def swap_masks(count):
     masks = [1 << bit for bit in range(count.bit_length() - 1)]
-    if 1 << len(masks) != count or len(masks) < 4:
+    if 1 << len(masks) != count or len(masks) < 3:
         return []
-    return [masks[-1:], [1, 2, 3]] + [[mask] for mask in masks[-2:1:-1]]
-
-
-def swap_sum(x, count, beside):
-    rounds = swap_rounds(count)
-    if not rounds:
-        return lax.psum(x, "space"), jnp.zeros_like(x), beside
-    for i, masks in enumerate(rounds):
-        others = [lax.ppermute(x, "space", [(j, j ^ mask) for j in range(count)]) for mask in masks]
-        if i == len(rounds) - 1:
-            return x, others[0], beside
-        x = x + others[0]
-        if len(others) == 3:
-            x = x + (others[1] + others[2])
+    return [mask | 1 for mask in [masks[-1], masks[1]] + masks[-2:1:-1]] + [1]
+
+
+def swap_sum(x, count, changed, put):
+    masks = swap_masks(count)
+    if not masks:
+        return lax.psum(x, "space"), jnp.zeros_like(x), put(changed)
+    for i, mask in enumerate(masks[:-1]):
+        x = x + lax.ppermute(x, "space", [(j, j ^ mask) for j in range(count)])
         if i == 0:
-            x, beside = lax.optimization_barrier((x, beside))
+            x, changed = lax.optimization_barrier((x, changed))
+        if i == len(masks) - 2:
+            x, product = lax.optimization_barrier((x, put(changed)))
+    return x, lax.ppermute(x, "space", [(j, j ^ masks[-1]) for j in range(count)]), product
 
 
 def remote_part(meta, space_tiles, forward, local, received):
@@ -397,8 +395,7 @@
     )
     share = remote_quad(v, quad, received)
     changed = remote_part(meta, space_tiles, forward, local, received)
-    x, y, changed = swap_sum(share, count, changed)
-    product = store(meta, changed, product)
+    x, y, product = swap_sum(share, count, changed, lambda rows: store(meta, rows, product))
     scale = 1.0 / math.sqrt(count * tile_rows * tile_nodes * species)
     return product.reshape(signal.shape), finish(x, y, scale)
 

time: 29.4 us -> 28.8 us (0.980)
  starting transfers between devices: 11.3 us -> 10.3 us
  waiting for transfers between devices: 7.91 us -> 8.3 us
    ppermute x5 -> x4, starting transfers between devices: 7.56 us -> 6.55 us  [the longest x3 6.06 us: swap_sum(): x = x + lax.ppermute(x, 'space', [(j, j ^ mask) for j in range(count)])]
    ppermute x5 -> x4, waiting for transfers between devices: 2.75 us -> 3.15 us  [the longest x3 2.33 us: swap_sum(): x = x + lax.ppermute(x, 'space', [(j, j ^ mask) for j in range(count)])]
  transfers between devices with their start and end apart: 8 -> 7, of which waited for: 5 -> 5; matrix products, arithmetic and copies ran while one was open for 0% -> 0% of each run, Pallas kernels for 25% -> 25%
where the time goes in v5:
time: 28.8 us; the launch traced here: 28.6 us
  starting transfers between devices  10.3 us (36%)
  Pallas kernels  9.29 us (32%)
  waiting for transfers between devices  8.3 us (29%)
  between operations  0.69 us (2%)
    ppermute x3, starting transfers between devices, swap_sum(): x = x + lax.ppermute(x, 'space', [(j, j ^ mask) for j in range(count)])  6.06 us
    pallas_call x1, Pallas kernels, local_part(): pl.pallas_call(kernel, out_shape=[pltpu.HBM(tiled.shape, jnp.float32), pl...  5.27 us
    ppermute x3, waiting for transfers between devices, on_device(): lax.ppermute(o, 'space', plan.route(leg))  5.16 us
    ppermute x3, starting transfers between devices, on_device(): lax.ppermute(o, 'space', plan.route(leg))  3.77 us
    ppermute x3, waiting for transfers between devices, swap_sum(): x = x + lax.ppermute(x, 'space', [(j, j ^ mask) for j in range(count)])  2.33 us
    pallas_call x1, Pallas kernels, pick(): pl.pallas_call(kernel, out_shape=[shape] * len(legs) + [pltpu.VMEM(tiled....  1.28 us
    pallas_call x1, Pallas kernels, remote_part(): pl.pallas_call(kernel, out_shape=pltpu.VMEM((own + BLOCK, nodes, species)...  1.02 us
    pallas_call x1, Pallas kernels, store(): pl.pallas_call(kernel, out_shape=pltpu.HBM(product.shape, jnp.float32), i...  0.97 us
  transfers between devices with their start and end apart: 7, of which 5 were waited for; matrix products, arithmetic and copies ran while one was open for 0% of the time, Pallas kernels for 25%

profile of v5, /device:TPU:0, one launch (start us, length us, event | category | flops | bytes accessed | tf_op | source)
XLA Modules:
  0.0 28.6 jit_solution(5516723271344315975)
XLA Ops:
  0.6 1.3 %pick.1 = (f32[8,64,128]{2,1,0:T(8,128)S(1)}, f32[8,64,128]{2,1,0:T(8,128)S(1)}, f32[8,64,128]{2,1,0:T(8,128)S(1)}, f32[32,64,128]{2,1,0:T(8,128)S(1)}) custom-call(s32[1,4,8]{2,1,0:T(4,128)} %lists_hbm.1, f32[32,64,128]{2,1,0:T(8,128)} %bitcast.3), custom_call_target="tpu_custom_call" | custom-call | tf_op jit(solution)/shard_map/pick/pallas_call | solution.py:124
  1.9 3.0 %collective-permute-start = (f32[8,64,128]{2,1,0:T(8,128)S(1)}, f32[8,64,128]{2,1,0:T(8,128)S(1)}, u32[]{:S(2)}, u32[]{:S(2)}) collective-permute-start(f32[8,64,128]{2,1,0:T(8,128)S(1)} %get-tuple-element.20), channel_id=1, source_target_pairs={{0,2},{2,0},{1,3},{3,1},{4,6},{6,4},{5,7},{7,5},{8,10},{10,8},{9,1... | collective-permute-start | bytes 786440 | tf_op jit(solution)/shard_map/ppermute | solution.py:392
  5.0 0.7 %collective-permute-start.1 = (f32[8,64,128]{2,1,0:T(8,128)S(1)}, f32[8,64,128]{2,1,0:T(8,128)S(1)}, u32[]{:S(2)}, u32[]{:S(2)}) collective-permute-start(f32[8,64,128]{2,1,0:T(8,128)S(1)} %get-tuple-element.21), channel_id=1, source_target_pairs={{2,4},{4,2},{3,5},{5,3},{6,8},{8,6},{7,9},{9,7},{10,12},{12,10},{1... | collective-permute-start | bytes 786440 | tf_op jit(solution)/shard_map/ppermute | solution.py:392
  5.6 0.1 collective-permute-start.2
  5.7 5.3 %local_part.1 = (f32[32,64,128]{2,1,0:T(8,128)}, f32[32,64,128]{2,1,0:T(8,128)S(1)}, f32[25,64,128]{2,1,0:T(8,128)S(1)}, f32[8,128]{1,0:T(8,128)S(1)}, s32[8,36]...) custom-call(s32[6,32]{1,0:T(8,128)} %bitcast.5, f32[32,64,128]{2,1,0:T(8,128)S(1)} %get-tuple-element.17.x_ref, ...), custom_call_target="tpu_custom_call" | custom-call | tf_op jit(solution)/shard_map/local_part/pallas_call | solution.py:231
  11.0 5.2 %collective-permute-done.rest_0_ = f32[8,64,128]{2,1,0:T(8,128)S(1)} collective-permute-done((f32[8,64,128]{2,1,0:T(8,128)S(1)}, f32[8,64,128]{2,1,0:T(8,128)S(1)}, u32[]{:S(2)}, u32[]{:S(2)}) %collective-permute-start) | collective-permute-done | bytes 262176 | tf_op jit(solution)/shard_map/ppermute | solution.py:392
  16.1 0.0 collective-permute-done.1.rest_1_
  16.1 0.0 collective-permute-done.2.rest_2_
  16.1 0.1 remote_quad.1
  16.2 2.2 %collective-permute-start.3 = (f32[1,128]{1,0:T(1,128)S(1)}, f32[1,128]{1,0:T(1,128)S(1)}, u32[]{:S(2)}, u32[]{:S(2)}) collective-permute-start(f32[1,128]{1,0:T(1,128)S(1)} %remote_quad.1), channel_id=1, source_target_pairs={{0,9},{1,8},{2,11},{3,10},{4,13},{5,12},{6,15},{7,14},{8,1},{9,0},... | collective-permute-start | bytes 1544 | tf_op jit(solution)/shard_map/ppermute | solution.py:292
  18.4 1.0 %remote_part.1.changed_ref = f32[36,64,128]{2,1,0:T(8,128)S(1)} custom-call(s32[8,36]{1,0:T(8,128)S(4)} %get-tuple-element.23.meta_ref, bf16[256,256]{1,0:T(8,128)(2,1)S(1)} %get-tuple-element.24.forward_ref, f32[32,64,384]{2,1,0:T(8,128)S(1)} %get-tuple-element.25.a_ref, f32[32,64,128]{2,1,0:T(8,128)S(1)} %get-tuple-element.26.p_ref, ...), custom_call_target="tpu_custom_call" | custom-call | tf_op jit(solution)/shard_map/remote_part/pallas_call | solution.py:327
  19.5 0.7 %collective-permute-done.3 = f32[1,128]{1,0:T(1,128)S(1)} collective-permute-done((f32[1,128]{1,0:T(1,128)S(1)}, f32[1,128]{1,0:T(1,128)S(1)}, u32[]{:S(2)}, u32[]{:S(2)}) %collective-permute-start.3) | collective-permute-done | bytes 544 | tf_op jit(solution)/shard_map/ppermute | solution.py:292
  20.2 2.2 %collective-permute-start.4 = (f32[1,128]{1,0:T(1,128)S(1)}, f32[1,128]{1,0:T(1,128)S(1)}, u32[]{:S(2)}, u32[]{:S(2)}) collective-permute-start(f32[1,128]{1,0:T(1,128)S(1)} %add.9), channel_id=1, source_target_pairs={{0,3},{1,2},{2,1},{3,0},{4,7},{5,6},{6,5},{7,4},{8,11},{9,10},{10,... | collective-permute-start | bytes 1544 | tf_op jit(solution)/shard_map/ppermute | solution.py:292
  22.3 1.3 %collective-permute-done.4 = f32[1,128]{1,0:T(1,128)S(1)} collective-permute-done((f32[1,128]{1,0:T(1,128)S(1)}, f32[1,128]{1,0:T(1,128)S(1)}, u32[]{:S(2)}, u32[]{:S(2)}) %collective-permute-start.4) | collective-permute-done | bytes 544 | tf_op jit(solution)/shard_map/ppermute | solution.py:292
  23.6 1.7 %collective-permute-start.5 = (f32[1,128]{1,0:T(1,128)S(1)}, f32[1,128]{1,0:T(1,128)S(1)}, u32[]{:S(2)}, u32[]{:S(2)}) collective-permute-start(f32[1,128]{1,0:T(1,128)S(1)} %add.10), channel_id=1, source_target_pairs={{0,5},{1,4},{2,7},{3,6},{4,1},{5,0},{6,3},{7,2},{8,13},{9,12},{10,... | collective-permute-start | bytes 1544 | tf_op jit(solution)/shard_map/ppermute | solution.py:292
  25.4 1.0 %store.1 = f32[32,64,128]{2,1,0:T(8,128)} custom-call(s32[8,36]{1,0:T(8,128)S(4)} %get-tuple-element.23.meta_ref, f32[36,64,128]{2,1,0:T(8,128)S(1)} %remote_part.1.changed_ref, f32[32,64,128]{2,1,0:T(8,128)} %get-tuple-element.29._), custom_call_target="tpu_custom_call", output_to_operand_aliasing={{}: (2, {})} | custom-call | tf_op jit(solution)/shard_map/store/pallas_call | solution.py:359
  26.3 0.3 %collective-permute-done.5 = f32[1,128]{1,0:T(1,128)S(1)} collective-permute-done((f32[1,128]{1,0:T(1,128)S(1)}, f32[1,128]{1,0:T(1,128)S(1)}, u32[]{:S(2)}, u32[]{:S(2)}) %collective-permute-start.5) | collective-permute-done | bytes 544 | tf_op jit(solution)/shard_map/ppermute | solution.py:292
  26.7 0.5 %collective-permute-start.6 = (f32[1,128]{1,0:T(1,128)S(1)}, f32[1,128]{1,0:T(1,128)S(1)}, u32[]{:S(2)}, u32[]{:S(2)}) collective-permute-start(f32[1,128]{1,0:T(1,128)S(1)} %add.11.x_ref), channel_id=1, source_target_pairs={{0,1},{1,0},{2,3},{3,2},{4,5},{5,4},{6,7},{7,6},{8,9},{9,8},{10,11... | collective-permute-start | bytes 1544 | tf_op jit(solution)/shard_map/ppermute | solution.py:297
  27.1 0.8 %collective-permute-done.6.y_ref = f32[1,128]{1,0:T(1,128)S(1)} collective-permute-done((f32[1,128]{1,0:T(1,128)S(1)}, f32[1,128]{1,0:T(1,128)S(1)}, u32[]{:S(2)}, u32[]{:S(2)}) %collective-permute-start.6) | collective-permute-done | bytes 544 | tf_op jit(solution)/shard_map/ppermute | solution.py:297
  28.0 0.6 %finish.1 = f32[1]{0:T(128)} custom-call(f32[1,128]{1,0:T(1,128)S(1)} %add.11.x_ref, f32[1,128]{1,0:T(1,128)S(1)} %collective-permute-done.6.y_ref), custom_call_target="tpu_custom_call" | custom-call | tf_op jit(solution)/shard_map/finish/pallas_call | solution.py:375
  (3 shorter events, 0.0 us)
Async XLA Ops:
  1.9 14.2 %collective-permute-start = (f32[8,64,128]{2,1,0:T(8,128)S(1)}, f32[8,64,128]{2,1,0:T(8,128)S(1)}, u32[]{:S(2)}, u32[]{:S(2)}) collective-permute-start(f32[8,64,128]{2,1,0:T(8,128)S(1)} %get-tuple-element.20), channel_id=1, source_target_pairs={{0,2},{2,0},{1,3},{3,1},{4,6},{6,4},{5,7},{7,5},{8,10},{10,8},{9,1... | collective-permute-start | bytes 786440 | tf_op jit(solution)/shard_map/ppermute | solution.py:392
  5.0 11.2 %collective-permute-start.1 = (f32[8,64,128]{2,1,0:T(8,128)S(1)}, f32[8,64,128]{2,1,0:T(8,128)S(1)}, u32[]{:S(2)}, u32[]{:S(2)}) collective-permute-start(f32[8,64,128]{2,1,0:T(8,128)S(1)} %get-tuple-element.21), channel_id=1, source_target_pairs={{2,4},{4,2},{3,5},{5,3},{6,8},{8,6},{7,9},{9,7},{10,12},{12,10},{1... | collective-permute-start | bytes 786440 | tf_op jit(solution)/shard_map/ppermute | solution.py:392
  5.6 10.5 %collective-permute-start.2 = (f32[8,64,128]{2,1,0:T(8,128)S(1)}, f32[8,64,128]{2,1,0:T(8,128)S(1)}, u32[]{:S(2)}, u32[]{:S(2)}) collective-permute-start(f32[8,64,128]{2,1,0:T(8,128)S(1)} %get-tuple-element.22), channel_id=1, source_target_pairs={{0,1},{1,0},{2,3},{3,2},{4,5},{5,4},{6,7},{7,6},{8,9},{9,8},{10,11... | collective-permute-start | bytes 786440 | tf_op jit(solution)/shard_map/ppermute | solution.py:392
  16.2 3.9 %collective-permute-start.3 = (f32[1,128]{1,0:T(1,128)S(1)}, f32[1,128]{1,0:T(1,128)S(1)}, u32[]{:S(2)}, u32[]{:S(2)}) collective-permute-start(f32[1,128]{1,0:T(1,128)S(1)} %remote_quad.1), channel_id=1, source_target_pairs={{0,9},{1,8},{2,11},{3,10},{4,13},{5,12},{6,15},{7,14},{8,1},{9,0},... | collective-permute-start | bytes 1544 | tf_op jit(solution)/shard_map/ppermute | solution.py:292
  20.2 3.4 %collective-permute-start.4 = (f32[1,128]{1,0:T(1,128)S(1)}, f32[1,128]{1,0:T(1,128)S(1)}, u32[]{:S(2)}, u32[]{:S(2)}) collective-permute-start(f32[1,128]{1,0:T(1,128)S(1)} %add.9), channel_id=1, source_target_pairs={{0,3},{1,2},{2,1},{3,0},{4,7},{5,6},{6,5},{7,4},{8,11},{9,10},{10,... | collective-permute-start | bytes 1544 | tf_op jit(solution)/shard_map/ppermute | solution.py:292
  23.6 3.0 %collective-permute-start.5 = (f32[1,128]{1,0:T(1,128)S(1)}, f32[1,128]{1,0:T(1,128)S(1)}, u32[]{:S(2)}, u32[]{:S(2)}) collective-permute-start(f32[1,128]{1,0:T(1,128)S(1)} %add.10), channel_id=1, source_target_pairs={{0,5},{1,4},{2,7},{3,6},{4,1},{5,0},{6,3},{7,2},{8,13},{9,12},{10,... | collective-permute-start | bytes 1544 | tf_op jit(solution)/shard_map/ppermute | solution.py:292
  26.7 1.3 %collective-permute-start.6 = (f32[1,128]{1,0:T(1,128)S(1)}, f32[1,128]{1,0:T(1,128)S(1)}, u32[]{:S(2)}, u32[]{:S(2)}) collective-permute-start(f32[1,128]{1,0:T(1,128)S(1)} %add.11.x_ref), channel_id=1, source_target_pairs={{0,1},{1,0},{2,3},{3,2},{4,5},{5,4},{6,7},{7,6},{8,9},{9,8},{10,11... | collective-permute-start | bytes 1544 | tf_op jit(solution)/shard_map/ppermute | solution.py:297

commit v6 on v5

--- a/solution.py
+++ b/solution.py
@@ -281,7 +281,7 @@
     masks = [1 << bit for bit in range(count.bit_length() - 1)]
     if 1 << len(masks) != count or len(masks) < 3:
         return []
-    return [mask | 1 for mask in [masks[-1], masks[1]] + masks[-2:1:-1]] + [1]
+    return [mask | 1 for mask in masks[2:-1] + [masks[1], masks[-1]]] + [1]
 
 
 def swap_sum(x, count, changed, put):

time: 28.8 us -> 28.8 us (level)
  no operation moved by 1% of the time
where the time goes in v6:
time: 28.8 us; the launch traced here: 28.6 us
  starting transfers between devices  10.2 us (35%)
  Pallas kernels  9.28 us (32%)
  waiting for transfers between devices  8.42 us (29%)
  between operations  0.69 us (2%)
    ppermute x3, starting transfers between devices, swap_sum(): x = x + lax.ppermute(x, 'space', [(j, j ^ mask) for j in range(count)])  5.95 us
    pallas_call x1, Pallas kernels, local_part(): pl.pallas_call(kernel, out_shape=[pltpu.HBM(tiled.shape, jnp.float32), pl...  5.27 us
    ppermute x3, waiting for transfers between devices, on_device(): lax.ppermute(o, 'space', plan.route(leg))  5.16 us
    ppermute x3, starting transfers between devices, on_device(): lax.ppermute(o, 'space', plan.route(leg))  3.77 us
    ppermute x3, waiting for transfers between devices, swap_sum(): x = x + lax.ppermute(x, 'space', [(j, j ^ mask) for j in range(count)])  2.44 us
    pallas_call x1, Pallas kernels, pick(): pl.pallas_call(kernel, out_shape=[shape] * len(legs) + [pltpu.VMEM(tiled....  1.28 us
    pallas_call x1, Pallas kernels, remote_part(): pl.pallas_call(kernel, out_shape=pltpu.VMEM((own + BLOCK, nodes, species)...  1.02 us
    pallas_call x1, Pallas kernels, store(): pl.pallas_call(kernel, out_shape=pltpu.HBM(product.shape, jnp.float32), i...  0.97 us
  transfers between devices with their start and end apart: 7, of which 5 were waited for; matrix products, arithmetic and copies ran while one was open for 0% of the time, Pallas kernels for 25%

profile of v6, /device:TPU:0, one launch (start us, length us, event | category | flops | bytes accessed | tf_op | source)
XLA Modules:
  0.0 28.6 jit_solution(9882248054542323031)
XLA Ops:
  0.6 1.3 %pick.1 = (f32[8,64,128]{2,1,0:T(8,128)S(1)}, f32[8,64,128]{2,1,0:T(8,128)S(1)}, f32[8,64,128]{2,1,0:T(8,128)S(1)}, f32[32,64,128]{2,1,0:T(8,128)S(1)}) custom-call(s32[1,4,8]{2,1,0:T(4,128)} %lists_hbm.1, f32[32,64,128]{2,1,0:T(8,128)} %bitcast.3), custom_call_target="tpu_custom_call" | custom-call | tf_op jit(solution)/shard_map/pick/pallas_call | solution.py:124
  1.9 3.0 %collective-permute-start = (f32[8,64,128]{2,1,0:T(8,128)S(1)}, f32[8,64,128]{2,1,0:T(8,128)S(1)}, u32[]{:S(2)}, u32[]{:S(2)}) collective-permute-start(f32[8,64,128]{2,1,0:T(8,128)S(1)} %get-tuple-element.20), channel_id=1, source_target_pairs={{0,2},{2,0},{1,3},{3,1},{4,6},{6,4},{5,7},{7,5},{8,10},{10,8},{9,1... | collective-permute-start | bytes 786440 | tf_op jit(solution)/shard_map/ppermute | solution.py:392
  5.0 0.7 %collective-permute-start.1 = (f32[8,64,128]{2,1,0:T(8,128)S(1)}, f32[8,64,128]{2,1,0:T(8,128)S(1)}, u32[]{:S(2)}, u32[]{:S(2)}) collective-permute-start(f32[8,64,128]{2,1,0:T(8,128)S(1)} %get-tuple-element.21), channel_id=1, source_target_pairs={{2,4},{4,2},{3,5},{5,3},{6,8},{8,6},{7,9},{9,7},{10,12},{12,10},{1... | collective-permute-start | bytes 786440 | tf_op jit(solution)/shard_map/ppermute | solution.py:392
  5.6 0.1 collective-permute-start.2
  5.7 5.3 %local_part.1 = (f32[32,64,128]{2,1,0:T(8,128)}, f32[32,64,128]{2,1,0:T(8,128)S(1)}, f32[25,64,128]{2,1,0:T(8,128)S(1)}, f32[8,128]{1,0:T(8,128)S(1)}, s32[8,36]...) custom-call(s32[6,32]{1,0:T(8,128)} %bitcast.5, f32[32,64,128]{2,1,0:T(8,128)S(1)} %get-tuple-element.17.x_ref, ...), custom_call_target="tpu_custom_call" | custom-call | tf_op jit(solution)/shard_map/local_part/pallas_call | solution.py:231
  11.0 5.2 %collective-permute-done.rest_0_ = f32[8,64,128]{2,1,0:T(8,128)S(1)} collective-permute-done((f32[8,64,128]{2,1,0:T(8,128)S(1)}, f32[8,64,128]{2,1,0:T(8,128)S(1)}, u32[]{:S(2)}, u32[]{:S(2)}) %collective-permute-start) | collective-permute-done | bytes 262176 | tf_op jit(solution)/shard_map/ppermute | solution.py:392
  16.1 0.0 collective-permute-done.1.rest_1_
  16.1 0.0 collective-permute-done.2.rest_2_
  16.1 0.1 remote_quad.1
  16.2 1.2 %collective-permute-start.3 = (f32[1,128]{1,0:T(1,128)S(1)}, f32[1,128]{1,0:T(1,128)S(1)}, u32[]{:S(2)}, u32[]{:S(2)}) collective-permute-start(f32[1,128]{1,0:T(1,128)S(1)} %remote_quad.1), channel_id=1, source_target_pairs={{0,5},{1,4},{2,7},{3,6},{4,1},{5,0},{6,3},{7,2},{8,13},{9,12},{10,... | collective-permute-start | bytes 1544 | tf_op jit(solution)/shard_map/ppermute | solution.py:292
  17.4 1.0 %remote_part.1.changed_ref = f32[36,64,128]{2,1,0:T(8,128)S(1)} custom-call(s32[8,36]{1,0:T(8,128)S(4)} %get-tuple-element.23.meta_ref, bf16[256,256]{1,0:T(8,128)(2,1)S(1)} %get-tuple-element.24.forward_ref, f32[32,64,384]{2,1,0:T(8,128)S(1)} %get-tuple-element.25.a_ref, f32[32,64,128]{2,1,0:T(8,128)S(1)} %get-tuple-element.26.p_ref, ...), custom_call_target="tpu_custom_call" | custom-call | tf_op jit(solution)/shard_map/remote_part/pallas_call | solution.py:327
  18.4 0.8 %collective-permute-done.3 = f32[1,128]{1,0:T(1,128)S(1)} collective-permute-done((f32[1,128]{1,0:T(1,128)S(1)}, f32[1,128]{1,0:T(1,128)S(1)}, u32[]{:S(2)}, u32[]{:S(2)}) %collective-permute-start.3) | collective-permute-done | bytes 544 | tf_op jit(solution)/shard_map/ppermute | solution.py:292
  19.3 2.0 %collective-permute-start.4 = (f32[1,128]{1,0:T(1,128)S(1)}, f32[1,128]{1,0:T(1,128)S(1)}, u32[]{:S(2)}, u32[]{:S(2)}) collective-permute-start(f32[1,128]{1,0:T(1,128)S(1)} %add.9), channel_id=1, source_target_pairs={{0,3},{1,2},{2,1},{3,0},{4,7},{5,6},{6,5},{7,4},{8,11},{9,10},{10,... | collective-permute-start | bytes 1544 | tf_op jit(solution)/shard_map/ppermute | solution.py:292
  21.3 1.3 %collective-permute-done.4 = f32[1,128]{1,0:T(1,128)S(1)} collective-permute-done((f32[1,128]{1,0:T(1,128)S(1)}, f32[1,128]{1,0:T(1,128)S(1)}, u32[]{:S(2)}, u32[]{:S(2)}) %collective-permute-start.4) | collective-permute-done | bytes 544 | tf_op jit(solution)/shard_map/ppermute | solution.py:292
  22.6 2.7 %collective-permute-start.5 = (f32[1,128]{1,0:T(1,128)S(1)}, f32[1,128]{1,0:T(1,128)S(1)}, u32[]{:S(2)}, u32[]{:S(2)}) collective-permute-start(f32[1,128]{1,0:T(1,128)S(1)} %add.10), channel_id=1, source_target_pairs={{0,9},{1,8},{2,11},{3,10},{4,13},{5,12},{6,15},{7,14},{8,1},{9,0},... | collective-permute-start | bytes 1544 | tf_op jit(solution)/shard_map/ppermute | solution.py:292
  25.4 1.0 %store.1 = f32[32,64,128]{2,1,0:T(8,128)} custom-call(s32[8,36]{1,0:T(8,128)S(4)} %get-tuple-element.23.meta_ref, f32[36,64,128]{2,1,0:T(8,128)S(1)} %remote_part.1.changed_ref, f32[32,64,128]{2,1,0:T(8,128)} %get-tuple-element.29._), custom_call_target="tpu_custom_call", output_to_operand_aliasing={{}: (2, {})} | custom-call | tf_op jit(solution)/shard_map/store/pallas_call | solution.py:359
  26.3 0.3 %collective-permute-done.5 = f32[1,128]{1,0:T(1,128)S(1)} collective-permute-done((f32[1,128]{1,0:T(1,128)S(1)}, f32[1,128]{1,0:T(1,128)S(1)}, u32[]{:S(2)}, u32[]{:S(2)}) %collective-permute-start.5) | collective-permute-done | bytes 544 | tf_op jit(solution)/shard_map/ppermute | solution.py:292
  26.7 0.5 %collective-permute-start.6 = (f32[1,128]{1,0:T(1,128)S(1)}, f32[1,128]{1,0:T(1,128)S(1)}, u32[]{:S(2)}, u32[]{:S(2)}) collective-permute-start(f32[1,128]{1,0:T(1,128)S(1)} %add.11.x_ref), channel_id=1, source_target_pairs={{0,1},{1,0},{2,3},{3,2},{4,5},{5,4},{6,7},{7,6},{8,9},{9,8},{10,11... | collective-permute-start | bytes 1544 | tf_op jit(solution)/shard_map/ppermute | solution.py:297
  27.1 0.8 %collective-permute-done.6.y_ref = f32[1,128]{1,0:T(1,128)S(1)} collective-permute-done((f32[1,128]{1,0:T(1,128)S(1)}, f32[1,128]{1,0:T(1,128)S(1)}, u32[]{:S(2)}, u32[]{:S(2)}) %collective-permute-start.6) | collective-permute-done | bytes 544 | tf_op jit(solution)/shard_map/ppermute | solution.py:297
  28.0 0.6 %finish.1 = f32[1]{0:T(128)} custom-call(f32[1,128]{1,0:T(1,128)S(1)} %add.11.x_ref, f32[1,128]{1,0:T(1,128)S(1)} %collective-permute-done.6.y_ref), custom_call_target="tpu_custom_call" | custom-call | tf_op jit(solution)/shard_map/finish/pallas_call | solution.py:375
  (3 shorter events, 0.0 us)
Async XLA Ops:
  1.9 14.2 %collective-permute-start = (f32[8,64,128]{2,1,0:T(8,128)S(1)}, f32[8,64,128]{2,1,0:T(8,128)S(1)}, u32[]{:S(2)}, u32[]{:S(2)}) collective-permute-start(f32[8,64,128]{2,1,0:T(8,128)S(1)} %get-tuple-element.20), channel_id=1, source_target_pairs={{0,2},{2,0},{1,3},{3,1},{4,6},{6,4},{5,7},{7,5},{8,10},{10,8},{9,1... | collective-permute-start | bytes 786440 | tf_op jit(solution)/shard_map/ppermute | solution.py:392
  5.0 11.2 %collective-permute-start.1 = (f32[8,64,128]{2,1,0:T(8,128)S(1)}, f32[8,64,128]{2,1,0:T(8,128)S(1)}, u32[]{:S(2)}, u32[]{:S(2)}) collective-permute-start(f32[8,64,128]{2,1,0:T(8,128)S(1)} %get-tuple-element.21), channel_id=1, source_target_pairs={{2,4},{4,2},{3,5},{5,3},{6,8},{8,6},{7,9},{9,7},{10,12},{12,10},{1... | collective-permute-start | bytes 786440 | tf_op jit(solution)/shard_map/ppermute | solution.py:392
  5.6 10.5 %collective-permute-start.2 = (f32[8,64,128]{2,1,0:T(8,128)S(1)}, f32[8,64,128]{2,1,0:T(8,128)S(1)}, u32[]{:S(2)}, u32[]{:S(2)}) collective-permute-start(f32[8,64,128]{2,1,0:T(8,128)S(1)} %get-tuple-element.22), channel_id=1, source_target_pairs={{0,1},{1,0},{2,3},{3,2},{4,5},{5,4},{6,7},{7,6},{8,9},{9,8},{10,11... | collective-permute-start | bytes 786440 | tf_op jit(solution)/shard_map/ppermute | solution.py:392
  16.2 3.0 %collective-permute-start.3 = (f32[1,128]{1,0:T(1,128)S(1)}, f32[1,128]{1,0:T(1,128)S(1)}, u32[]{:S(2)}, u32[]{:S(2)}) collective-permute-start(f32[1,128]{1,0:T(1,128)S(1)} %remote_quad.1), channel_id=1, source_target_pairs={{0,5},{1,4},{2,7},{3,6},{4,1},{5,0},{6,3},{7,2},{8,13},{9,12},{10,... | collective-permute-start | bytes 1544 | tf_op jit(solution)/shard_map/ppermute | solution.py:292
  19.3 3.3 %collective-permute-start.4 = (f32[1,128]{1,0:T(1,128)S(1)}, f32[1,128]{1,0:T(1,128)S(1)}, u32[]{:S(2)}, u32[]{:S(2)}) collective-permute-start(f32[1,128]{1,0:T(1,128)S(1)} %add.9), channel_id=1, source_target_pairs={{0,3},{1,2},{2,1},{3,0},{4,7},{5,6},{6,5},{7,4},{8,11},{9,10},{10,... | collective-permute-start | bytes 1544 | tf_op jit(solution)/shard_map/ppermute | solution.py:292
  22.6 4.0 %collective-permute-start.5 = (f32[1,128]{1,0:T(1,128)S(1)}, f32[1,128]{1,0:T(1,128)S(1)}, u32[]{:S(2)}, u32[]{:S(2)}) collective-permute-start(f32[1,128]{1,0:T(1,128)S(1)} %add.10), channel_id=1, source_target_pairs={{0,9},{1,8},{2,11},{3,10},{4,13},{5,12},{6,15},{7,14},{8,1},{9,0},... | collective-permute-start | bytes 1544 | tf_op jit(solution)/shard_map/ppermute | solution.py:292
  26.7 1.3 %collective-permute-start.6 = (f32[1,128]{1,0:T(1,128)S(1)}, f32[1,128]{1,0:T(1,128)S(1)}, u32[]{:S(2)}, u32[]{:S(2)}) collective-permute-start(f32[1,128]{1,0:T(1,128)S(1)} %add.11.x_ref), channel_id=1, source_target_pairs={{0,1},{1,0},{2,3},{3,2},{4,5},{5,4},{6,7},{7,6},{8,9},{9,8},{10,11... | collective-permute-start | bytes 1544 | tf_op jit(solution)/shard_map/ppermute | solution.py:297
